TPU v7x, 128 devices: a whole 4x4x4 slice. The times are simulated.
128 devices in a mesh: segment: 4 (over x_lo, core), dp: 32 (over z, y, x_hi).
Axes of the slice: x: 4 (x_hi: 2, x_lo: 2; x = x_hi * 2 + x_lo), y: 4, z: 4, core: 2. Of those that a mesh axis runs over, the one named last changes fastest.
Arguments:
- latents: bfloat16 [2, 4096, 1280], P(None, 'dp'), may hold values from -6 to 6
- cotangent: bfloat16 [2, 4096, 1280], P(None, 'dp'), may hold values from -6 to 6
- timesteps: int32 [2, 32], P(None, 'dp'), may hold values from 0 to 999
- time_table: bfloat16 [4, 1000, 1280], P('segment'), may hold values from -3 to 3
- w_in: bfloat16 [4, 1280, 1280], P('segment'), may hold values from -0.15625 to 0.15625
- w_out: bfloat16 [4, 1280, 1280], P('segment'), may hold values from -0.15625 to 0.15625
- w_skip: bfloat16 [4, 1280, 1280], P('segment'), may hold values from -0.15625 to 0.15625
Outputs:
- phase_out: bfloat16 [4, 2, 4096, 1280], P('segment', None, 'dp')
- input_grads: bfloat16 [4, 2, 4096, 1280], P('segment', None, 'dp')
- grad_w_in: float32 [4, 1280, 1280], P('segment', 'dp')
- grad_w_out: float32 [4, 1280, 1280], P('segment', 'dp')
- grad_w_skip: float32 [4, 1280, 1280], P('segment', 'dp')
All inputs are finite; a program needn't handle non-finite values.
Results may differ from a plain program's by a relative error of at most 0.028.
Values may be sent and summed in bfloat16 or wider, within the bound.
A program may use at most 128 MiB of HBM per device.

v0:
```python
import jax
import jax.numpy as jnp
from jax import lax
from jax.sharding import PartitionSpec as P


def passed_along(x, axis, by):
    devices = lax.axis_size(axis)
    pairs = [(i, i + by) for i in range(devices) if 0 <= i + by < devices]
    return lax.ppermute(x, axis, pairs)


def silu_grad(pre):
    sig = jax.nn.sigmoid(pre)
    return sig * (1.0 + pre * (1.0 - sig))


def store(buffer, slot, valid, value):
    return buffer.at[slot].set(jnp.where(valid, value, buffer[slot]))


def send_forward(output, skip_out, phase_id, last, with_mirror):
    received = None
    arriving, near_skip = passed_along((output, skip_out), "segment", 1)
    if with_mirror:
        far_skip = passed_along(skip_out, "segment", 3)
        received = jnp.where(phase_id == last, far_skip, near_skip)
    return (arriving, received)


def send_backward(d_in, d_skip, phase_id, with_mirror):
    received = None
    arriving, near_grad = passed_along((d_in, d_skip), "segment", -1)
    if with_mirror:
        far_grad = passed_along(d_skip, "segment", -3)
        received = jnp.where(phase_id == 0, far_grad, near_grad)
    return (arriving, received)


def body(latents, cotangent, timesteps, time_table, w_in, w_out, w_skip):
    phase_id = lax.axis_index("segment")
    last = lax.axis_size("segment") - 1
    is_up = phase_id >= 2
    micro = latents.shape[0]
    rows = latents.shape[1]
    width = latents.shape[2]
    w_first = w_in[0]
    w_second = w_out[0]
    w_side = w_skip[0]
    embed = time_table[0][timesteps[:, 0]].astype(jnp.float32)
    zeros_act = jnp.zeros((rows, width), jnp.bfloat16)
    inputs_buf = jnp.zeros((micro, rows, width), jnp.bfloat16)
    pre_buf = jnp.zeros((micro, rows, width), jnp.float32)
    gated_buf = jnp.zeros((micro, rows, width), jnp.bfloat16)
    output_buf = jnp.zeros((micro, rows, width), jnp.bfloat16)
    left_buf = jnp.zeros((micro, rows, width), jnp.bfloat16)
    skip_buf = jnp.zeros((micro, rows, width), jnp.bfloat16)
    arriving = zeros_act
    for tick in range(micro + 3):
        index = tick - phase_id
        valid = (index >= 0) & (index < micro)
        slot = jnp.clip(index, 0, micro - 1)
        block_in = jnp.where(phase_id == 0, latents[slot], arriving)
        skip_in = skip_buf[slot]
        bias = embed[slot][None, :]
        pre = (
            jnp.dot(block_in, w_first, preferred_element_type=jnp.float32)
            + jnp.dot(skip_in, w_side, preferred_element_type=jnp.float32)
            + bias
        )
        gated = jax.nn.silu(pre).astype(jnp.bfloat16)
        output = (
            block_in.astype(jnp.float32)
            + jnp.dot(gated, w_second, preferred_element_type=jnp.float32)
        ).astype(jnp.bfloat16)
        skip_out = jnp.dot(output, w_side, preferred_element_type=jnp.float32).astype(jnp.bfloat16)
        left = jnp.where(is_up, skip_in, output)
        inputs_buf = store(inputs_buf, slot, valid, block_in)
        pre_buf = store(pre_buf, slot, valid, pre)
        gated_buf = store(gated_buf, slot, valid, gated)
        output_buf = store(output_buf, slot, valid, output)
        left_buf = store(left_buf, slot, valid, left)
        if tick < micro + 2:
            arriving, received = send_forward(output, skip_out, phase_id, last, tick < micro + 1)
            if tick < micro + 1:
                target = tick - (last - phase_id)
                usable = is_up & (target >= 0) & (target < micro)
                skip_buf = store(skip_buf, jnp.clip(target, 0, micro - 1), usable, received)
    dskip_buf = jnp.zeros((micro, rows, width), jnp.bfloat16)
    grad_in_buf = jnp.zeros((micro, rows, width), jnp.bfloat16)
    grad_first = jnp.zeros((width, width), jnp.float32)
    grad_second = jnp.zeros((width, width), jnp.float32)
    grad_side = jnp.zeros((width, width), jnp.float32)
    arriving = zeros_act
    for tick in range(micro + 3):
        index = tick - (last - phase_id)
        valid = (index >= 0) & (index < micro)
        slot = jnp.clip(index, 0, micro - 1)
        upstream = jnp.where(phase_id == last, cotangent[slot], arriving)
        pre = pre_buf[slot]
        gated = gated_buf[slot]
        block_in = inputs_buf[slot]
        left = left_buf[slot]
        dskip_in = dskip_buf[slot]
        total = (
            upstream.astype(jnp.float32)
            + jnp.dot(dskip_in, w_side.T, preferred_element_type=jnp.float32)
        ).astype(jnp.bfloat16)
        d_pre = (
            jnp.dot(total, w_second.T, preferred_element_type=jnp.float32) * silu_grad(pre)
        ).astype(jnp.bfloat16)
        d_skip = jnp.dot(d_pre, w_side.T, preferred_element_type=jnp.float32).astype(jnp.bfloat16)
        d_in = (
            total.astype(jnp.float32)
            + jnp.dot(d_pre, w_first.T, preferred_element_type=jnp.float32)
        ).astype(jnp.bfloat16)
        right = jnp.where(is_up, d_pre, dskip_in)
        grad_first = jnp.where(
            valid,
            grad_first + jnp.dot(block_in.T, d_pre, preferred_element_type=jnp.float32),
            grad_first,
        )
        grad_second = jnp.where(
            valid,
            grad_second + jnp.dot(gated.T, total, preferred_element_type=jnp.float32),
            grad_second,
        )
        grad_side = jnp.where(
            valid, grad_side + jnp.dot(left.T, right, preferred_element_type=jnp.float32), grad_side
        )
        grad_in_buf = store(grad_in_buf, slot, valid, d_in)
        if tick < micro + 2:
            arriving, received = send_backward(d_in, d_skip, phase_id, tick < micro + 1)
            if tick < micro + 1:
                target = tick - phase_id
                usable = jnp.logical_not(is_up) & (target >= 0) & (target < micro)
                dskip_buf = store(dskip_buf, jnp.clip(target, 0, micro - 1), usable, received)
    grad_first, grad_second, grad_side = (
        lax.psum_scatter(
            grad_first.astype(jnp.bfloat16), "dp", scatter_dimension=0, tiled=True
        ).astype(jnp.float32),
        lax.psum_scatter(
            grad_second.astype(jnp.bfloat16), "dp", scatter_dimension=0, tiled=True
        ).astype(jnp.float32),
        lax.psum_scatter(
            grad_side.astype(jnp.bfloat16), "dp", scatter_dimension=0, tiled=True
        ).astype(jnp.float32),
    )
    return (
        output_buf[None],
        grad_in_buf[None],
        grad_first[None],
        grad_second[None],
        grad_side[None],
    )


def solution(mesh):
    in_specs = (
        P(None, "dp", None),
        P(None, "dp", None),
        P(None, "dp"),
        P("segment", None, None),
        P("segment", None, None),
        P("segment", None, None),
        P("segment", None, None),
    )
    out_specs = (
        P("segment", None, "dp", None),
        P("segment", None, "dp", None),
        P("segment", "dp", None),
        P("segment", "dp", None),
        P("segment", "dp", None),
    )
    return jax.shard_map(body, mesh=mesh, in_specs=in_specs, out_specs=out_specs, check_vma=False)
```

profile of v0, /device:TPU:0, one launch (start us, length us, event | category | flops | bytes accessed | tf_op | source)
XLA Modules:
  0.0 778.8 jit_solution(16473135019007040589)
XLA Ops:
  8.1 2.7 gather_fusion
  10.8 3.4 fusion.65
  16.2 3.8 bitcast_dynamic-update-slice_fusion
  20.1 2.2 bitcast_dynamic-update-slice_fusion.1
  22.4 2.5 fusion.165
  24.9 3.7 collective-permute-start.1
  28.6 2.0 collective-permute-start.2
  30.6 2.0 collective-permute-start
  33.5 2.4 select_dynamic-update-slice_fusion
  35.9 1.7 constant_dynamic-slice_fusion.11
  37.7 2.0 constant_dynamic-slice_fusion.20
  40.5 2.4 bitcast_dynamic-update-slice_fusion.7
  42.9 2.0 constant_dynamic-slice_fusion.3
  46.5 3.3 fusion.159
  49.9 1.9 bitcast_dynamic-update-slice_fusion.6
  52.5 1.5 fusion.243
  54.0 2.4 fusion.211
  57.1 1.4 collective-permute-start.3
  64.0 4.6 collective-permute-done.4
  68.6 2.3 fusion.225
  71.6 1.6 fusion.242
  73.2 2.3 fusion.210
  76.1 2.7 collective-permute-start.6
  79.5 2.7 collective-permute-start.7
  82.2 2.9 collective-permute-start.8
  88.3 2.0 collective-permute-done.7
  90.3 2.4 fusion.224
  94.4 1.5 fusion.241
  95.9 2.2 fusion.209
  98.1 2.2 fusion.223
  100.3 3.9 collective-permute-start.9
  109.5 2.1 fusion.208
  111.6 2.5 fusion.153
  118.0 1.9 bitcast_dynamic-update-slice_fusion.4
  121.2 2.2 bitcast_dynamic-update-slice_fusion.5
  128.1 2.4 fusion.150
  133.1 1.5 collective-permute-start.15
  135.6 1.8 fusion.251
  138.8 5.9 collective-permute-done.14
  146.8 2.4 fusion.147
  154.1 1.8 fusion.248
  157.2 1.5 collective-permute-done.17
  159.9 4.0 collective-permute-done.16
  165.1 2.4 fusion.144
  167.6 1.9 fusion.245
  171.8 6.0 collective-permute-done.19
  179.8 2.3 fusion.141
  182.8 2.7 fusion.14
  185.9 2.0 bitcast_dynamic-update-slice_fusion.2
  187.9 2.1 fusion.234
  197.3 2.8 fusion.13
  200.4 2.2 convolution_select_fusion.2
  202.5 2.1 fusion.11
  204.6 2.1 fusion.10
  206.8 2.1 fusion.9
  208.8 3.8 fusion.12
  212.7 2.0 copy.41
  214.6 3.7 fusion.216
  218.4 168.8 %reduce-scatter.8.cloned.1.call-done = bf16[40,1280]{1,0:T(8,128)(2,1)} async-done(((bf16[1280,1280]{1,0:T(8,128)(2,1)}), bf16[40,1280]{1,0:T(8,128)(2,1)}) %reduce-scatter.8.cloned.1.call-update) | async-done | bytes 102416 | tf_op jit(solution)/shard_map/reduce_scatter | solution.py:145
  387.2 1.6 bitcast_convert_fusion
  388.8 189.9 %reduce-scatter.6.cloned.1.call-done = bf16[40,1280]{1,0:T(8,128)(2,1)} async-done(((bf16[1280,1280]{1,0:T(8,128)(2,1)}), bf16[40,1280]{1,0:T(8,128)(2,1)}) %reduce-scatter.6.cloned.1.call-update) | async-done | bytes 102416 | tf_op jit(solution)/shard_map/reduce_scatter | solution.py:142
  578.6 1.6 bitcast_convert_fusion.1
  580.2 190.2 %reduce-scatter.4.cloned.1.call-done = bf16[40,1280]{1,0:T(8,128)(2,1)} async-done(((bf16[1280,1280]{1,0:T(8,128)(2,1)}), bf16[40,1280]{1,0:T(8,128)(2,1)}) %reduce-scatter.4.cloned.1.call-update) | async-done | bytes 102416 | tf_op jit(solution)/shard_map/reduce_scatter | solution.py:139
  770.4 1.6 bitcast_convert_fusion.2
  (188 shorter events, 63.1 us)
Async XLA Ops:
  7.2 9.1 %copy-start = (bf16[1,1280,1280]{2,1,0:T(8,128)(2,1)S(1)}, bf16[1,1280,1280]{2,1,0:T(8,128)(2,1)}, u32[]{:S(2)}) copy-start(bf16[1,1280,1280]{2,1,0:T(8,128)(2,1)} %param.83) | copy-start | bytes 9830404
  7.2 7.1 copy-start.41
  7.2 380.0 %reduce-scatter.8.cloned.1.call-start = ((), (), s32[]{:S(2)}) async-start(), calls=%async_computation.5 | async-start | bytes 3379200 | tf_op jit(solution)/shard_map/reduce_scatter | solution.py:145
  16.2 3.9 copy-start.6
  16.2 3.9 copy-start.42
  20.1 2.3 copy-start.29
  20.1 2.2 copy-start.1
  22.4 2.5 copy-start.3
  24.9 24.9 %collective-permute-start.1 = (bf16[128,1280]{1,0:T(8,128)(2,1)}, bf16[128,1280]{1,0:T(8,128)(2,1)}, u32[]{:S(2)}, u32[]{:S(2)}) collective-permute-start(bf16[128,1280]{1,0:T(8,128)(2,1)} %fusion.165), channel_id=1, source_target_pairs={{0,96},{1,97},{2,98},{3,99},{4,100},{5,101},{6,102},{7,103},{8,104... | collective-permute-start | bytes 983048 | tf_op jit(solution)/shard_map/ppermute | solution.py:10
  28.6 21.2 %collective-permute-start.2 = (bf16[128,1280]{1,0:T(8,128)(2,1)}, bf16[128,1280]{1,0:T(8,128)(2,1)}, u32[]{:S(2)}, u32[]{:S(2)}) collective-permute-start(bf16[128,1280]{1,0:T(8,128)(2,1)} %fusion.165), channel_id=1, source_target_pairs={{0,32},{32,64},{64,96},{1,33},{33,65},{65,97},{2,34},{34,66},{66,9... | collective-permute-start | bytes 983048 | tf_op jit(solution)/shard_map/ppermute | solution.py:10
  30.6 21.8 %collective-permute-start = (bf16[128,1280]{1,0:T(8,128)(2,1)}, bf16[128,1280]{1,0:T(8,128)(2,1)}, u32[]{:S(2)}, u32[]{:S(2)}) collective-permute-start(bf16[128,1280]{1,0:T(8,128)(2,1)} %get-tuple-element.479), channel_id=1, source_target_pairs={{0,32},{32,64},{64,96},{1,33},{33,65},{65,97},{2,34},{34,66},{66,9... | collective-permute-start | bytes 983048 | tf_op jit(solution)/shard_map/ppermute | solution.py:10
  46.5 5.3 copy-start.2
  49.8 68.2 %copy-start.14 = (bf16[128,1280]{1,0:T(8,128)(2,1)}, bf16[128,1280]{1,0:T(8,128)(2,1)S(1)}, u32[]{:S(2)}) copy-start(bf16[128,1280]{1,0:T(8,128)(2,1)S(1)} %fusion.159) | copy-start | bytes 983044
  49.8 2.7 copy-start.7
  49.8 2.7 copy-start.39
  49.9 4.1 copy-start.28
  54.0 2.4 copy-start.43
  56.4 2.8 copy-start.30
  57.1 11.6 %copy-start.4 = (bf16[2,128,1280]{2,1,0:T(8,128)(2,1)S(1)}, bf16[2,128,1280]{2,1,0:T(8,128)(2,1)}, u32[]{:S(2)}) copy-start(bf16[2,128,1280]{2,1,0:T(8,128)(2,1)} %copy-done.3) | copy-start | bytes 1966084
  57.1 11.6 %copy-start.37 = (bf16[1,128,1280]{2,1,0:T(8,128)(2,1)S(1)}, bf16[1,128,1280]{2,1,0:T(8,128)(2,1)}, u32[]{:S(2)}) copy-start(bf16[1,128,1280]{2,1,0:T(8,128)(2,1)} %get-tuple-element.495) | copy-start | bytes 983044
  57.1 11.6 %copy-start.38 = (bf16[1,128,1280]{2,1,0:T(8,128)(2,1)S(1)}, bf16[1,128,1280]{2,1,0:T(8,128)(2,1)}, u32[]{:S(2)}) copy-start(bf16[1,128,1280]{2,1,0:T(8,128)(2,1)} %get-tuple-element.496) | copy-start | bytes 983044
  57.1 14.5 %collective-permute-start.3 = (bf16[128,1280]{1,0:T(8,128)(2,1)S(1)}, bf16[128,1280]{1,0:T(8,128)(2,1)S(1)}, u32[]{:S(2)}, u32[]{:S(2)}) collective-permute-start(bf16[128,1280]{1,0:T(8,128)(2,1)S(1)} %add_convert_fusion.11), channel_id=1, source_target_pairs={{0,32},{32,64},{64,96},{1,33},{33,65},{65,97},{2,34},{34,66},{66,9... | collective-permute-start | bytes 983048 | tf_op jit(solution)/shard_map/ppermute | solution.py:10
  59.2 9.4 %collective-permute-start.4 = (bf16[128,1280]{1,0:T(8,128)(2,1)S(1)}, bf16[128,1280]{1,0:T(8,128)(2,1)S(1)}, u32[]{:S(2)}, u32[]{:S(2)}) collective-permute-start(bf16[128,1280]{1,0:T(8,128)(2,1)S(1)} %fusion.168), channel_id=1, source_target_pairs={{0,96},{1,97},{2,98},{3,99},{4,100},{5,101},{6,102},{7,103},{8,104... | collective-permute-start | bytes 983048 | tf_op jit(solution)/shard_map/ppermute | solution.py:10
  60.5 8.1 %collective-permute-start.5 = (bf16[128,1280]{1,0:T(8,128)(2,1)S(1)}, bf16[128,1280]{1,0:T(8,128)(2,1)S(1)}, u32[]{:S(2)}, u32[]{:S(2)}) collective-permute-start(bf16[128,1280]{1,0:T(8,128)(2,1)S(1)} %fusion.168), channel_id=1, source_target_pairs={{0,32},{32,64},{64,96},{1,33},{33,65},{65,97},{2,34},{34,66},{66,9... | collective-permute-start | bytes 983048 | tf_op jit(solution)/shard_map/ppermute | solution.py:10
  75.4 4.0 copy-start.31
  76.1 18.2 %collective-permute-start.6 = (bf16[128,1280]{1,0:T(8,128)(2,1)S(1)}, bf16[128,1280]{1,0:T(8,128)(2,1)S(1)}, u32[]{:S(2)}, u32[]{:S(2)}) collective-permute-start(bf16[128,1280]{1,0:T(8,128)(2,1)S(1)} %add_convert_fusion.10), channel_id=1, source_target_pairs={{0,32},{32,64},{64,96},{1,33},{33,65},{65,97},{2,34},{34,66},{66,9... | collective-permute-start | bytes 983048 | tf_op jit(solution)/shard_map/ppermute | solution.py:10
  79.5 10.9 %collective-permute-start.7 = (bf16[128,1280]{1,0:T(8,128)(2,1)S(1)}, bf16[128,1280]{1,0:T(8,128)(2,1)S(1)}, u32[]{:S(2)}, u32[]{:S(2)}) collective-permute-start(bf16[128,1280]{1,0:T(8,128)(2,1)S(1)} %fusion.171), channel_id=1, source_target_pairs={{0,96},{1,97},{2,98},{3,99},{4,100},{5,101},{6,102},{7,103},{8,104... | collective-permute-start | bytes 983048 | tf_op jit(solution)/shard_map/ppermute | solution.py:10
  82.2 8.1 %collective-permute-start.8 = (bf16[128,1280]{1,0:T(8,128)(2,1)S(1)}, bf16[128,1280]{1,0:T(8,128)(2,1)S(1)}, u32[]{:S(2)}, u32[]{:S(2)}) collective-permute-start(bf16[128,1280]{1,0:T(8,128)(2,1)S(1)} %fusion.171), channel_id=1, source_target_pairs={{0,32},{32,64},{64,96},{1,33},{33,65},{65,97},{2,34},{34,66},{66,9... | collective-permute-start | bytes 983048 | tf_op jit(solution)/shard_map/ppermute | solution.py:10
  98.1 2.2 copy-start.33
  100.3 7.8 %collective-permute-start.9 = (bf16[128,1280]{1,0:T(8,128)(2,1)S(1)}, bf16[128,1280]{1,0:T(8,128)(2,1)S(1)}, u32[]{:S(2)}, u32[]{:S(2)}) collective-permute-start(bf16[128,1280]{1,0:T(8,128)(2,1)S(1)} %get-tuple-element.480), channel_id=1, source_target_pairs={{0,32},{32,64},{64,96},{1,33},{33,65},{65,97},{2,34},{34,66},{66,9... | collective-permute-start | bytes 983048 | tf_op jit(solution)/shard_map/ppermute | solution.py:10
  111.6 9.6 %copy-start.35 = (f32[128,1280]{1,0:T(8,128)}, f32[128,1280]{1,0:T(8,128)S(1)}, u32[]{:S(2)}) copy-start(f32[128,1280]{1,0:T(8,128)S(1)} %get-tuple-element.492) | copy-start | bytes 1966084
  114.2 10.9 %copy-start.8 = (bf16[128,1280]{1,0:T(8,128)(2,1)}, bf16[128,1280]{1,0:T(8,128)(2,1)S(1)}, u32[]{:S(2)}) copy-start(bf16[128,1280]{1,0:T(8,128)(2,1)S(1)} %fusion.153) | copy-start | bytes 983044
  115.4 10.7 %collective-permute-start.11 = (bf16[128,1280]{1,0:T(8,128)(2,1)S(1)}, bf16[128,1280]{1,0:T(8,128)(2,1)S(1)}, u32[]{:S(2)}, u32[]{:S(2)}) collective-permute-start(bf16[128,1280]{1,0:T(8,128)(2,1)S(1)} %fusion.174), channel_id=1, source_target_pairs={{96,0},{97,1},{98,2},{99,3},{100,4},{101,5},{102,6},{103,7},{104,8... | collective-permute-start | bytes 983048 | tf_op jit(solution)/shard_map/ppermute | solution.py:10
  116.7 9.4 %collective-permute-start.12 = (bf16[128,1280]{1,0:T(8,128)(2,1)S(1)}, bf16[128,1280]{1,0:T(8,128)(2,1)S(1)}, u32[]{:S(2)}, u32[]{:S(2)}) collective-permute-start(bf16[128,1280]{1,0:T(8,128)(2,1)S(1)} %fusion.174), channel_id=1, source_target_pairs={{32,0},{64,32},{96,64},{33,1},{65,33},{97,65},{34,2},{66,34},{98,6... | collective-permute-start | bytes 983048 | tf_op jit(solution)/shard_map/ppermute | solution.py:10
  119.9 7.0 collective-permute-start.10
  125.0 1.9 copy-start.13
  128.1 7.5 copy-start.16
  130.6 5.1 copy-start.9
  131.8 13.0 %collective-permute-start.14 = (bf16[128,1280]{1,0:T(8,128)(2,1)S(1)}, bf16[128,1280]{1,0:T(8,128)(2,1)S(1)}, u32[]{:S(2)}, u32[]{:S(2)}) collective-permute-start(bf16[128,1280]{1,0:T(8,128)(2,1)S(1)} %fusion.177), channel_id=1, source_target_pairs={{96,0},{97,1},{98,2},{99,3},{100,4},{101,5},{102,6},{103,7},{104,8... | collective-permute-start | bytes 983048 | tf_op jit(solution)/shard_map/ppermute | solution.py:10
  133.1 11.7 %collective-permute-start.15 = (bf16[128,1280]{1,0:T(8,128)(2,1)S(1)}, bf16[128,1280]{1,0:T(8,128)(2,1)S(1)}, u32[]{:S(2)}, u32[]{:S(2)}) collective-permute-start(bf16[128,1280]{1,0:T(8,128)(2,1)S(1)} %fusion.177), channel_id=1, source_target_pairs={{32,0},{64,32},{96,64},{33,1},{65,33},{97,65},{34,2},{66,34},{98,6... | collective-permute-start | bytes 983048 | tf_op jit(solution)/shard_map/ppermute | solution.py:10
  137.5 8.1 %collective-permute-start.13 = (bf16[128,1280]{1,0:T(8,128)(2,1)S(1)}, bf16[128,1280]{1,0:T(8,128)(2,1)S(1)}, u32[]{:S(2)}, u32[]{:S(2)}) collective-permute-start(bf16[128,1280]{1,0:T(8,128)(2,1)S(1)} %get-tuple-element.465), channel_id=1, source_target_pairs={{32,0},{64,32},{96,64},{33,1},{65,33},{97,65},{34,2},{66,34},{98,6... | collective-permute-start | bytes 983048 | tf_op jit(solution)/shard_map/ppermute | solution.py:10
  146.8 7.3 copy-start.18
  149.2 4.9 copy-start.11
  150.4 8.4 %collective-permute-start.17 = (bf16[128,1280]{1,0:T(8,128)(2,1)S(1)}, bf16[128,1280]{1,0:T(8,128)(2,1)S(1)}, u32[]{:S(2)}, u32[]{:S(2)}) collective-permute-start(bf16[128,1280]{1,0:T(8,128)(2,1)S(1)} %fusion.180), channel_id=1, source_target_pairs={{96,0},{97,1},{98,2},{99,3},{100,4},{101,5},{102,6},{103,7},{104,8... | collective-permute-start | bytes 983048 | tf_op jit(solution)/shard_map/ppermute | solution.py:10
  151.7 7.4 collective-permute-start.18
  155.9 8.0 %collective-permute-start.16 = (bf16[128,1280]{1,0:T(8,128)(2,1)S(1)}, bf16[128,1280]{1,0:T(8,128)(2,1)S(1)}, u32[]{:S(2)}, u32[]{:S(2)}) collective-permute-start(bf16[128,1280]{1,0:T(8,128)(2,1)S(1)} %get-tuple-element.463), channel_id=1, source_target_pairs={{32,0},{64,32},{96,64},{33,1},{65,33},{97,65},{34,2},{66,34},{98,6... | collective-permute-start | bytes 983048 | tf_op jit(solution)/shard_map/ppermute | solution.py:10
  165.1 2.5 copy-start.22
  167.6 4.2 copy-start.26
  169.4 12.6 %copy-start.5 = (bf16[2,128,1280]{2,1,0:T(8,128)(2,1)}, bf16[2,128,1280]{2,1,0:T(8,128)(2,1)S(1)}, u32[]{:S(2)}) copy-start(bf16[2,128,1280]{2,1,0:T(8,128)(2,1)S(1)} %get-tuple-element.460) | copy-start | bytes 1966084
  169.4 8.4 %collective-permute-start.19 = (bf16[128,1280]{1,0:T(8,128)(2,1)S(1)}, bf16[128,1280]{1,0:T(8,128)(2,1)S(1)}, u32[]{:S(2)}, u32[]{:S(2)}) collective-permute-start(bf16[128,1280]{1,0:T(8,128)(2,1)S(1)} %get-tuple-element.461), channel_id=1, source_target_pairs={{32,0},{64,32},{96,64},{33,1},{65,33},{97,65},{34,2},{66,34},{98,6... | collective-permute-start | bytes 983048 | tf_op jit(solution)/shard_map/ppermute | solution.py:10
  185.5 393.1 %reduce-scatter.6.cloned.1.call-start = ((), (), s32[]{:S(2)}) async-start(), calls=%async_computation.4 | async-start | bytes 3379200 | tf_op jit(solution)/shard_map/reduce_scatter | solution.py:142
  185.8 4.3 copy-start.32
  185.8 5.3 copy-start.34
  187.9 4.2 copy-start.36
  190.0 2.9 copy-start.15
  192.9 1.1 copy-start.17
  194.0 1.1 copy-start.19
  195.1 1.1 copy-start.23
  196.2 1.1 copy-start.25
  200.0 570.3 %reduce-scatter.4.cloned.1.call-start = ((), (), s32[]{:S(2)}) async-start(), calls=%async_computation.3 | async-start | bytes 3379200 | tf_op jit(solution)/shard_map/reduce_scatter | solution.py:139
  200.3 2.2 copy-start.10
  202.5 2.1 copy-start.12
  204.6 2.1 copy-start.27
  206.7 2.1 copy-start.21
  (3 other events, 2.3 us)
Sparse Core Ops, SparseCore 0:
  185.7 201.4 reduce-scatter.7
  389.7 188.8 reduce-scatter.5
  581.0 189.3 reduce-scatter.3
where the time goes:
time: 788 us; the launch traced here: 779 us
  waiting for transfers between devices  573 us (73%)
  matrix products  91.3 us (12%)
  starting transfers between devices  37.6 us (5%)
  other arithmetic  35.3 us (4%)
  local copies, waits for them, and re-layouts  26 us (3%)
  between operations  15.2 us (2%)
    reduce_scatter x1, waiting for transfers between devices, body(): lax.psum_scatter(grad_first.astype(jnp.bfloat16), 'dp', scatter_dimension...  190 us
    reduce_scatter x1, waiting for transfers between devices, body(): lax.psum_scatter(grad_second.astype(jnp.bfloat16), 'dp', scatter_dimensio...  190 us
    reduce_scatter x1, waiting for transfers between devices, body(): lax.psum_scatter(grad_side.astype(jnp.bfloat16), 'dp', scatter_dimension=...  169 us
    ppermute x20, starting transfers between devices, passed_along(): return lax.ppermute(x, axis, pairs)  37 us
    scatter x18, other arithmetic, store(): return buffer.at[slot].set(jnp.where(valid, value, buffer[slot]))  27.4 us
    ppermute x20, waiting for transfers between devices, passed_along(): return lax.ppermute(x, axis, pairs)  24.5 us
  transfers between devices with their start and end apart: 23, of which 10 were waited for; matrix products, arithmetic and copies ran while one was open for 11% of the time, Pallas kernels for 0%

commit v1 on v0

v1 whole, which is shorter than its diff:
```python
import jax
import jax.numpy as jnp
from jax import lax
from jax.experimental import pallas as pl
from jax.experimental.pallas import tpu as pltpu
from jax.sharding import PartitionSpec as P

MESH = pl.DeviceIdType.MESH
F32 = jnp.float32
BF16 = jnp.bfloat16
C = 1280
R = 128
TILE = 256
NT = (((1,), (1,)), ((), ()))
SPLITS = (
    ((0, 384, 0, 1), (384, 256, 0, -1), (640, 256, 1, 1), (896, 384, 1, -1)),
    ((0, 256, 0, 1), (256, 384, 0, -1), (640, 384, 1, 1), (1024, 256, 1, -1)),
    ((0, 384, 0, 1), (384, 256, 0, -1), (640, 256, 1, 1), (896, 384, 1, -1)),
)
BLOCKS = tuple((k, n, *block) for k in range(3) for n, block in enumerate(SPLITS[k]))


def kernel(
    lat, cot, bias, w_in, w_out, w_skip,
    po, gi, g_in, g_out, g_skip,
    w1, w2, w3, x, up, sk, dk, pre, gat, tot, dpre, lt, grads, r1, r2, r3, s1, q1, q2, q3, xs, xr,
    wsem, x_s, x_r, sk_s, sk_r, up_s, up_r, dk_s, dk_r, rs_s, rs_r, xh_s, xh_r,
):
    s = lax.axis_index("segment")
    dp = lax.axis_index("dp")
    z = dp // 8
    y = (dp // 2) % 4
    xh = dp % 2

    def along(axis, by):
        if axis == 0:
            return ((z + by + 4) % 4) * 8 + y * 2 + xh
        return z * 8 + ((y + by + 4) % 4) * 2 + xh

    partner = z * 8 + y * 2 + (1 - xh)
    loads = [
        pltpu.make_async_copy(src, dst, wsem.at[n])
        for n, (src, dst) in enumerate(((w_in, w1), (w_out, w2), (w_skip, w3)))
    ]
    x_load = pltpu.make_async_copy(lat, x, x_r.at[2])
    up_load = pltpu.make_async_copy(cot, up, up_r.at[2])

    @pl.when(s == 0)
    def _():
        x_load.start()

    for load in loads:
        load.start()

    @pl.when(s == 3)
    def _():
        up_load.start()

    barrier = pltpu.get_barrier_semaphore()
    for by in (1, 2, 3):
        pl.semaphore_signal(barrier, inc=1, device_id={"segment": (s + by) % 4}, device_id_type=MESH)
    for other in (along(0, 1), along(0, -1), along(1, 1), along(1, -1), partner):
        pl.semaphore_signal(barrier, inc=1, device_id={"dp": other}, device_id_type=MESH)
    pl.semaphore_wait(barrier, 8)

    def hand(buf, dst, m, send, recv, to):
        rows = pl.ds(pl.multiple_of(m * R, R), R)
        return pltpu.make_async_remote_copy(
            src_ref=buf.at[rows], dst_ref=dst.at[rows], send_sem=send.at[m], recv_sem=recv.at[m],
            device_id={"segment": to}, device_id_type=MESH,
        )

    def send_x(m):
        return hand(po, x, m, x_s, x_r, (s + 1) % 4)

    def send_sk(m):
        return hand(sk, sk, m, sk_s, sk_r, 3 - s)

    def send_up(m):
        return hand(gi, up, m, up_s, up_r, (s + 3) % 4)

    def send_dk(m):
        return hand(dk, dk, m, dk_s, dk_r, 3 - s)

    columns = [pl.ds(n * TILE, TILE) for n in range(C // TILE)]
    on3 = s // 3

    @pl.loop(0, 4)
    def _(i):
        kind = on3 * (i % 2) + (1 - on3) * (i // 2)
        m = on3 * (i // 2) + (1 - on3) * (i % 2)
        rows = pl.ds(pl.multiple_of(m * R, R), R)

        @pl.when(kind == 0)
        def _():
            @pl.when((s == 0) & (m == 0))
            def _():
                x_load.wait()

            @pl.when(s > 0)
            def _():
                send_x(m).wait_recv()

            @pl.when(i == 0)
            def _():
                loads[0].wait()

            for n in columns:
                pre[rows, n] = (
                    jnp.dot(x[rows, :], w1[:, n], preferred_element_type=F32) + bias[m, :, n]
                )

            @pl.when(i == 0)
            def _():
                loads[1].wait()
                loads[2].wait()

            @pl.when(s >= 2)
            def _():
                send_sk(m).wait_recv()
                for n in columns:
                    pre[rows, n] += jnp.dot(sk[rows, :], w3[:, n], preferred_element_type=F32)

            for n in columns:
                v = pre[rows, n]
                g = 1.0 / (1.0 + jnp.exp(-v))
                gat[rows, n] = (v * g).astype(BF16)
                pre[rows, n] = g * (1.0 + v * (1.0 - g))
            for n in columns:
                po[rows, n] = (
                    x[rows, n].astype(F32)
                    + jnp.dot(gat[rows, :], w2[:, n], preferred_element_type=F32)
                ).astype(BF16)

            @pl.when(s < 3)
            def _():
                send_x(m).start()

            @pl.when(s < 2)
            def _():
                for n in columns:
                    sk[rows, n] = jnp.dot(
                        po[rows, :], w3[:, n], preferred_element_type=F32
                    ).astype(BF16)
                send_sk(m).start()

        @pl.when(kind == 1)
        def _():
            @pl.when((s == 3) & (m == 0))
            def _():
                up_load.wait()

            @pl.when(s < 3)
            def _():
                send_up(m).wait_recv()

            @pl.when(s < 2)
            def _():
                send_dk(m).wait_recv()
                for n in columns:
                    tot[rows, n] = (
                        up[rows, n].astype(F32)
                        + lax.dot_general(dk[rows, :], w3[n, :], NT, preferred_element_type=F32)
                    ).astype(BF16)

            @pl.when(s >= 2)
            def _():
                tot[rows, :] = up[rows, :]

            for n in columns:
                dpre[rows, n] = (
                    lax.dot_general(tot[rows, :], w2[n, :], NT, preferred_element_type=F32)
                    * pre[rows, n]
                ).astype(BF16)
            for n in columns:
                gi[rows, n] = (
                    tot[rows, n].astype(F32)
                    + lax.dot_general(dpre[rows, :], w1[n, :], NT, preferred_element_type=F32)
                ).astype(BF16)

            @pl.when(s > 0)
            def _():
                send_up(m).start()

            @pl.when(s >= 2)
            def _():
                for n in columns:
                    dk[rows, n] = lax.dot_general(
                        dpre[rows, :], w3[n, :], NT, preferred_element_type=F32
                    ).astype(BF16)
                send_dk(m).start()

        @pl.when(kind == on3)
        def _():
            for n in columns:
                lt[0, n, rows] = x[rows, n].T
                lt[1, n, rows] = gat[rows, n].T

            @pl.when(s < 2)
            def _():
                for n in columns:
                    lt[2, n, rows] = po[rows, n].T

            @pl.when(s >= 2)
            def _():
                for n in columns:
                    lt[2, n, rows] = sk[rows, n].T

    def ring(stage, msg, block, src, dst, axis, by):
        n = block[0] * 4 + block[1]
        return pltpu.make_async_remote_copy(
            src_ref=src, dst_ref=dst, send_sem=rs_s.at[stage, msg, n], recv_sem=rs_r.at[stage, msg, n],
            device_id={"dp": along(axis, by)}, device_id_type=MESH,
        )

    def piece(block, pos):
        k, _, col, width, colour, _ = block
        cols = pl.ds(col, width)
        if colour == 0:
            return grads.at[k, pos % 4, :, :, cols]
        return grads.at[k, :, pos % 4, :, cols]

    def first(block, msg):
        k, _, col, width, colour, by = block
        cols = pl.ds(col, width)
        pos = (z, y)[colour]
        if msg == 0:
            return ring(0, 0, block, piece(block, pos + 2), r1.at[k, :, :, cols], colour, by)
        if msg == 1:
            return ring(0, 1, block, r1.at[k, :, :, cols], r2.at[k, :, :, cols], colour, by)
        return ring(0, 2, block, piece(block, pos - by + 4), r3.at[k, :, :, cols], colour, -by)

    def second(block, msg):
        k, _, col, width, colour, by = block
        cols = pl.ds(col, width)
        pos = (y, z)[colour]
        axis = 1 - colour
        if msg == 0:
            return ring(1, 0, block, s1.at[k, (pos + 2) % 4, :, cols], q1.at[k, :, cols], axis, by)
        if msg == 1:
            return ring(1, 1, block, q1.at[k, :, cols], q2.at[k, :, cols], axis, by)
        return ring(1, 2, block, s1.at[k, (pos - by + 4) % 4, :, cols], q3.at[k, :, cols], axis, -by)

    def product(k, right):
        @pl.loop(0, 4)
        def _(zp):
            left = lt[k, pl.ds(pl.multiple_of(zp * 320, 320), 320), :]
            for n in columns:
                acc = jnp.dot(left, right[:, n], preferred_element_type=F32).astype(BF16)
                for yp in range(4):
                    grads[k, zp, yp, :, n] = acc[yp * 80 : (yp + 1) * 80]

    for k in (1, 2, 0):
        if k == 2:

            @pl.when(s < 2)
            def _():
                product(2, dk)

            @pl.when(s >= 2)
            def _():
                product(2, dpre)
        else:
            product(k, (dpre, tot)[k])
        for block in BLOCKS[4 * k : 4 * k + 4]:
            first(block, 0).start()
            first(block, 2).start()
    order = BLOCKS[4:12] + BLOCKS[:4]
    for block in order:
        k, _, col, width, colour, by = block
        cols = pl.ds(col, width)
        first(block, 0).wait_recv()
        pos = (z, y)[colour] + by + 4
        r1[k, :, :, cols] = (
            r1[k, :, :, cols].astype(F32) + piece(block, pos)[...].astype(F32)
        ).astype(BF16)
        first(block, 1).start()
    for block in order:
        k, _, col, width, colour, by = block
        cols = pl.ds(col, width)
        first(block, 1).wait_recv()
        first(block, 2).wait_recv()
        s1[k, :, :, cols] = (
            piece(block, (z, y)[colour])[...].astype(F32)
            + r2[k, :, :, cols].astype(F32)
            + r3[k, :, :, cols].astype(F32)
        ).astype(BF16)
        second(block, 0).start()
        second(block, 2).start()
    for block in order:
        k, _, col, width, colour, by = block
        cols = pl.ds(col, width)
        second(block, 0).wait_recv()
        pos = ((y, z)[colour] + by + 4) % 4
        q1[k, :, cols] = (q1[k, :, cols].astype(F32) + s1[k, pos, :, cols].astype(F32)).astype(BF16)
        second(block, 1).start()

    def pair(k):
        return pltpu.make_async_remote_copy(
            src_ref=xs.at[k, 1 - xh], dst_ref=xr.at[k], send_sem=xh_s.at[k], recv_sem=xh_r.at[k],
            device_id={"dp": partner}, device_id_type=MESH,
        )

    for block in order:
        k, last, col, width, colour, by = block
        cols = pl.ds(col, width)
        second(block, 1).wait_recv()
        second(block, 2).wait_recv()
        part = (
            s1[k, (y, z)[colour], :, cols].astype(F32)
            + q2[k, :, cols].astype(F32)
            + q3[k, :, cols].astype(F32)
        )
        xs[k, 0, :, cols] = part[:40].astype(BF16)
        xs[k, 1, :, cols] = part[40:].astype(BF16)
        if last == 3:
            pair(k).start()
    for k in (1, 2, 0):
        pair(k).wait_recv()
        (g_in, g_out, g_skip)[k][...] = xs[k, xh].astype(F32) + xr[k].astype(F32)
    for block in order:
        for msg in range(3):
            first(block, msg).wait_send()
            second(block, msg).wait_send()
    for k in range(3):
        pair(k).wait_send()
    for m in range(2):

        @pl.when(s < 3)
        def _():
            send_x(m).wait_send()

        @pl.when(s < 2)
        def _():
            send_sk(m).wait_send()

        @pl.when(s > 0)
        def _():
            send_up(m).wait_send()

        @pl.when(s >= 2)
        def _():
            send_dk(m).wait_send()


def body(latents, cotangent, timesteps, time_table, w_in, w_out, w_skip):
    rows = 2 * R
    bias = time_table[0][timesteps[:, 0]].astype(F32)[:, None, :]
    vmem = pl.BlockSpec(memory_space=pltpu.VMEM)
    hbm = pl.BlockSpec(memory_space=pl.ANY)
    act = pltpu.VMEM((rows, C), BF16)
    weight = pltpu.VMEM((C, C), BF16)
    quarter = pltpu.VMEM((3, 4, 80, C), BF16)
    sixteenth = pltpu.VMEM((3, 80, C), BF16)
    dma = pltpu.SemaphoreType.DMA
    out_act = jax.ShapeDtypeStruct((rows, C), BF16)
    out_grad = jax.ShapeDtypeStruct((40, C), F32)
    po, gi, g_in, g_out, g_skip = pl.pallas_call(
        kernel,
        name="window",
        out_shape=(out_act, out_act, out_grad, out_grad, out_grad),
        in_specs=[hbm, hbm, vmem, hbm, hbm, hbm],
        out_specs=[vmem] * 5,
        scratch_shapes=[
            weight, weight, weight,
            act, act, act, act,
            pltpu.VMEM((rows, C), F32),
            act, act, act,
            pltpu.VMEM((3, C, rows), BF16),
            pltpu.VMEM((3, 4, 4, 80, C), BF16),
            quarter, quarter, quarter, quarter,
            sixteenth, sixteenth, sixteenth,
            pltpu.VMEM((3, 2, 40, C), BF16),
            pltpu.VMEM((3, 40, C), BF16),
            dma((3,)),
            dma((2,)), dma((3,)),
            dma((2,)), dma((2,)),
            dma((2,)), dma((3,)),
            dma((2,)), dma((2,)),
            dma((2, 3, 12)), dma((2, 3, 12)),
            dma((3,)), dma((3,)),
        ],
        compiler_params=pltpu.CompilerParams(
            collective_id=0, has_side_effects=True, vmem_limit_bytes=60 * 1024 * 1024
        ),
    )(
        latents.reshape(rows, C), cotangent.reshape(rows, C), bias,
        w_in.reshape(C, C), w_out.reshape(C, C), w_skip.reshape(C, C),
    )
    return (
        po.reshape(1, 2, R, C),
        gi.reshape(1, 2, R, C),
        g_in[None],
        g_out[None],
        g_skip[None],
    )


def solution(mesh):
    in_specs = (
        P(None, "dp", None),
        P(None, "dp", None),
        P(None, "dp"),
        P("segment", None, None),
        P("segment", None, None),
        P("segment", None, None),
        P("segment", None, None),
    )
    out_specs = (
        P("segment", None, "dp", None),
        P("segment", None, "dp", None),
        P("segment", "dp", None),
        P("segment", "dp", None),
        P("segment", "dp", None),
    )
    return jax.shard_map(body, mesh=mesh, in_specs=in_specs, out_specs=out_specs, check_vma=False)
```

time: 788 us -> 138 us (0.18); the launches traced: 779 us -> 138 us
  waiting for transfers between devices: 573 us -> 0 us
  Pallas kernels: 0 us -> 126 us
  matrix products: 91.3 us -> 0 us
  starting transfers between devices: 37.6 us -> 0 us
  other arithmetic: 35.3 us -> 0.67 us
  local copies, waits for them, and re-layouts: 26 us -> 10.8 us
  between operations: 15.2 us -> 0.66 us
    reduce_scatter x3 -> x0, waiting for transfers between devices: 549 us -> none  [the longest x1 190 us: body(): lax.psum_scatter(grad_first.astype(jnp.bfloat16), 'dp', scatter_dimension...]
    pallas_call x0 -> x1, Pallas kernels: none -> 126 us  [body(): pl.pallas_call(kernel, name='window', out_shape=(out_act, out_act, out_gr...]
    dot_general x51 -> x0, matrix products: 91.3 us -> none  [the longest x5 12.8 us: body(): jnp.dot(block_in, w_first, preferred_element_type=jnp.float32)]
    ppermute x20 -> x0, starting transfers between devices: 37 us -> none  [passed_along(): return lax.ppermute(x, axis, pairs)]
    scatter x18 -> x0, other arithmetic: 27.4 us -> none  [store(): return buffer.at[slot].set(jnp.where(valid, value, buffer[slot]))]
    ppermute x20 -> x0, waiting for transfers between devices: 24.5 us -> none  [passed_along(): return lax.ppermute(x, axis, pairs)]
    dynamic_slice x26 -> x0, local copies, waits for them, and re-layouts: 14.6 us -> none  [the longest x25 14.5 us: store(): return buffer.at[slot].set(jnp.where(valid, value, buffer[slot]))]
  transfers between devices with their start and end apart: 23 -> 0, of which waited for: 10 -> 0; matrix products, arithmetic and copies ran while one was open for 11% -> 0% of each run, Pallas kernels for 0% -> 0%
where the time goes in v1:
time: 138 us
  Pallas kernels  126 us (91%)
  local copies, waits for them, and re-layouts  10.8 us (8%)
    pallas_call x1, Pallas kernels, body(): pl.pallas_call(kernel, name='window', out_shape=(out_act, out_act, out_gr...  126 us
    unnamed x9, local copies, waits for them, and re-layouts  9.62 us

profile of v1, /device:TPU:0, one launch (start us, length us, event | category | flops | bytes accessed | tf_op | source)
XLA Modules:
  0.0 138.1 jit_solution(17516410718698622623)
XLA Ops:
  0.6 0.0 copy-start
  0.6 1.7 %copy-done = bf16[1,1000,1280]{2,1,0:T(8,128)(2,1)S(1)} copy-done((bf16[1,1000,1280]{2,1,0:T(8,128)(2,1)S(1)}, bf16[1,1000,1280]{2,1,0:T(8,128)(2,1)}, u32[]{:S(2)}) %copy-start) | copy-done | bytes 2560024
  2.4 0.7 fusion
  3.0 0.6 gather_fusion
  3.6 0.6 reshape.47.bias
  4.2 126.0 %window.1 = (bf16[256,1280]{1,0:T(8,128)(2,1)}, bf16[256,1280]{1,0:T(8,128)(2,1)}, f32[40,1280]{1,0:T(8,128)}, f32[40,1280]{1,0:T(8,128)}, f32[40,1280]{1,0:T(8,128)}) custom-call(bf16[256,1280]{1,0:T(8,128)(2,1)} %bitcast.19, bf16[256,1280]{1,0:T(8,128)(2,1)} %bitcast.20, f32[2,1,1280]{2,1,0:T(1,128)} %reshape.47.bias, bf16[1280,1280]{1,0:T(8,128)(2,1)} %bitcast.14, ...), custom_call_target="tpu_custom_call" | custom-call | tf_op jit(solution)/shard_map/window/pallas_call | solution.py:358
  130.2 0.0 copy-start.1
  130.2 2.0 %copy.17 = bf16[1,2,128,1280]{3,2,1,0:T(8,128)(2,1)} copy(bf16[1,2,128,1280]{3,2,1,0:T(8,128)(2,1)} %bitcast.18) | data formatting | bytes 1310720
  132.2 2.0 %copy.18 = bf16[1,2,128,1280]{3,2,1,0:T(8,128)(2,1)} copy(bf16[1,2,128,1280]{3,2,1,0:T(8,128)(2,1)} %bitcast.17) | data formatting | bytes 1310720
  134.1 1.6 %copy.19 = f32[1,40,1280]{2,1,0:T(8,128)} copy(f32[1,40,1280]{2,1,0:T(8,128)} %bitcast.23) | data formatting | bytes 409600
  135.8 1.6 %copy.20 = f32[1,40,1280]{2,1,0:T(8,128)} copy(f32[1,40,1280]{2,1,0:T(8,128)} %bitcast.22) | data formatting | bytes 409600
  137.4 0.0 copy-done.1
  137.4 0.7 copy.21
  (1 shorter events, 0.0 us)
Async XLA Ops:
  0.6 1.7 %copy-start = (bf16[1,1000,1280]{2,1,0:T(8,128)(2,1)S(1)}, bf16[1,1000,1280]{2,1,0:T(8,128)(2,1)}, u32[]{:S(2)}) copy-start(bf16[1,1000,1280]{2,1,0:T(8,128)(2,1)} %param.10) | copy-start | bytes 7680004
  130.2 7.2 %copy-start.1 = (f32[40,1280]{1,0:T(8,128)S(1)}, f32[40,1280]{1,0:T(8,128)}, u32[]{:S(2)}) copy-start(f32[40,1280]{1,0:T(8,128)} %get-tuple-element.14) | copy-start | bytes 614404

commit v2 on v1

--- a/solution.py
+++ b/solution.py
@@ -21,10 +21,10 @@
 
 
 def kernel(
-    lat, cot, bias, w_in, w_out, w_skip,
+    lat, cot, steps, table, w_in, w_out, w_skip,
     po, gi, g_in, g_out, g_skip,
-    w1, w2, w3, x, up, sk, dk, pre, gat, tot, dpre, lt, grads, r1, r2, r3, s1, q1, q2, q3, xs, xr,
-    wsem, x_s, x_r, sk_s, sk_r, up_s, up_r, dk_s, dk_r, rs_s, rs_r, xh_s, xh_r,
+    w1, w2, w3, bias, x, up, sk, dk, pre, gat, tot, dpre, lt, grads, r1, r2, r3, s1, q1, q2, q3, xs, xr,
+    wsem, turn, x_s, x_r, sk_s, sk_r, up_s, up_r, dk_s, dk_r, rs_s, rs_r, xh_s, xh_r,
 ):
     s = lax.axis_index("segment")
     dp = lax.axis_index("dp")
@@ -61,6 +61,12 @@
         pl.semaphore_signal(barrier, inc=1, device_id={"segment": (s + by) % 4}, device_id_type=MESH)
     for other in (along(0, 1), along(0, -1), along(1, 1), along(1, -1), partner):
         pl.semaphore_signal(barrier, inc=1, device_id={"dp": other}, device_id_type=MESH)
+    row = lax.broadcasted_iota(jnp.int32, (8, table.shape[0]), 0)
+    chosen = jnp.where(row == 0, steps[0, 0], steps[1, 0])
+    hot = lax.broadcasted_iota(jnp.int32, (8, table.shape[0]), 1) == chosen
+    found = jnp.dot(hot.astype(F32).astype(BF16), table[...], preferred_element_type=F32)
+    bias[0] = found[0:1]
+    bias[1] = found[1:2]
     pl.semaphore_wait(barrier, 8)
 
     def hand(buf, dst, m, send, recv, to):
@@ -84,127 +90,6 @@
 
     columns = [pl.ds(n * TILE, TILE) for n in range(C // TILE)]
     on3 = s // 3
-
-    @pl.loop(0, 4)
-    def _(i):
-        kind = on3 * (i % 2) + (1 - on3) * (i // 2)
-        m = on3 * (i // 2) + (1 - on3) * (i % 2)
-        rows = pl.ds(pl.multiple_of(m * R, R), R)
-
-        @pl.when(kind == 0)
-        def _():
-            @pl.when((s == 0) & (m == 0))
-            def _():
-                x_load.wait()
-
-            @pl.when(s > 0)
-            def _():
-                send_x(m).wait_recv()
-
-            @pl.when(i == 0)
-            def _():
-                loads[0].wait()
-
-            for n in columns:
-                pre[rows, n] = (
-                    jnp.dot(x[rows, :], w1[:, n], preferred_element_type=F32) + bias[m, :, n]
-                )
-
-            @pl.when(i == 0)
-            def _():
-                loads[1].wait()
-                loads[2].wait()
-
-            @pl.when(s >= 2)
-            def _():
-                send_sk(m).wait_recv()
-                for n in columns:
-                    pre[rows, n] += jnp.dot(sk[rows, :], w3[:, n], preferred_element_type=F32)
-
-            for n in columns:
-                v = pre[rows, n]
-                g = 1.0 / (1.0 + jnp.exp(-v))
-                gat[rows, n] = (v * g).astype(BF16)
-                pre[rows, n] = g * (1.0 + v * (1.0 - g))
-            for n in columns:
-                po[rows, n] = (
-                    x[rows, n].astype(F32)
-                    + jnp.dot(gat[rows, :], w2[:, n], preferred_element_type=F32)
-                ).astype(BF16)
-
-            @pl.when(s < 3)
-            def _():
-                send_x(m).start()
-
-            @pl.when(s < 2)
-            def _():
-                for n in columns:
-                    sk[rows, n] = jnp.dot(
-                        po[rows, :], w3[:, n], preferred_element_type=F32
-                    ).astype(BF16)
-                send_sk(m).start()
-
-        @pl.when(kind == 1)
-        def _():
-            @pl.when((s == 3) & (m == 0))
-            def _():
-                up_load.wait()
-
-            @pl.when(s < 3)
-            def _():
-                send_up(m).wait_recv()
-
-            @pl.when(s < 2)
-            def _():
-                send_dk(m).wait_recv()
-                for n in columns:
-                    tot[rows, n] = (
-                        up[rows, n].astype(F32)
-                        + lax.dot_general(dk[rows, :], w3[n, :], NT, preferred_element_type=F32)
-                    ).astype(BF16)
-
-            @pl.when(s >= 2)
-            def _():
-                tot[rows, :] = up[rows, :]
-
-            for n in columns:
-                dpre[rows, n] = (
-                    lax.dot_general(tot[rows, :], w2[n, :], NT, preferred_element_type=F32)
-                    * pre[rows, n]
-                ).astype(BF16)
-            for n in columns:
-                gi[rows, n] = (
-                    tot[rows, n].astype(F32)
-                    + lax.dot_general(dpre[rows, :], w1[n, :], NT, preferred_element_type=F32)
-                ).astype(BF16)
-
-            @pl.when(s > 0)
-            def _():
-                send_up(m).start()
-
-            @pl.when(s >= 2)
-            def _():
-                for n in columns:
-                    dk[rows, n] = lax.dot_general(
-                        dpre[rows, :], w3[n, :], NT, preferred_element_type=F32
-                    ).astype(BF16)
-                send_dk(m).start()
-
-        @pl.when(kind == on3)
-        def _():
-            for n in columns:
-                lt[0, n, rows] = x[rows, n].T
-                lt[1, n, rows] = gat[rows, n].T
-
-            @pl.when(s < 2)
-            def _():
-                for n in columns:
-                    lt[2, n, rows] = po[rows, n].T
-
-            @pl.when(s >= 2)
-            def _():
-                for n in columns:
-                    lt[2, n, rows] = sk[rows, n].T
 
     def ring(stage, msg, block, src, dst, axis, by):
         n = block[0] * 4 + block[1]
@@ -250,22 +135,184 @@
                 for yp in range(4):
                     grads[k, zp, yp, :, n] = acc[yp * 80 : (yp + 1) * 80]
 
-    for k in (1, 2, 0):
-        if k == 2:
-
-            @pl.when(s < 2)
-            def _():
-                product(2, dk)
-
-            @pl.when(s >= 2)
-            def _():
-                product(2, dpre)
-        else:
-            product(k, (dpre, tot)[k])
+    def begin(k):
         for block in BLOCKS[4 * k : 4 * k + 4]:
             first(block, 0).start()
             first(block, 2).start()
-    order = BLOCKS[4:12] + BLOCKS[:4]
+
+    @pl.loop(0, 4)
+    def _(i):
+        kind = on3 * (i % 2) + (1 - on3) * (i // 2)
+        m = on3 * (i // 2) + (1 - on3) * (i % 2)
+        rows = pl.ds(pl.multiple_of(m * R, R), R)
+
+        @pl.when(kind == 0)
+        def _():
+            @pl.when((s == 0) & (m == 0))
+            def _():
+                x_load.wait()
+
+            @pl.when(s > 0)
+            def _():
+                send_x(m).wait_recv()
+
+            @pl.when(i == 0)
+            def _():
+                loads[0].wait()
+
+            for n in columns:
+                pre[rows, n] = jnp.dot(x[rows, :], w1[:, n], preferred_element_type=F32)
+
+            @pl.when(i == 0)
+            def _():
+                loads[1].wait()
+                loads[2].wait()
+
+            @pl.when(s >= 2)
+            def _():
+                send_sk(m).wait_recv()
+                for n in columns:
+                    pre[rows, n] += jnp.dot(sk[rows, :], w3[:, n], preferred_element_type=F32)
+
+            for n in columns:
+                v = pre[rows, n] + bias[m, :, n]
+                g = 1.0 / (1.0 + jnp.exp(-v))
+                gat[rows, n] = (v * g).astype(BF16)
+                pre[rows, n] = g * (1.0 + v * (1.0 - g))
+            for n in columns:
+                po[rows, n] = (
+                    x[rows, n].astype(F32)
+                    + jnp.dot(gat[rows, :], w2[:, n], preferred_element_type=F32)
+                ).astype(BF16)
+
+            @pl.when(s < 3)
+            def _():
+                send_x(m).start()
+
+            @pl.when(s < 2)
+            def _():
+                for n in columns:
+                    sk[rows, n] = jnp.dot(
+                        po[rows, :], w3[:, n], preferred_element_type=F32
+                    ).astype(BF16)
+
+                @pl.when(s == 1)
+                def _():
+                    send_sk(m).start()
+
+                    @pl.when(m == 1)
+                    def _():
+                        for j in range(2):
+                            send_x(j).wait_send()
+                            send_sk(j).wait_send()
+                        pl.semaphore_signal(turn, inc=1, device_id={"segment": 0}, device_id_type=MESH)
+
+                @pl.when(s == 0)
+                def _():
+                    @pl.when(m == 1)
+                    def _():
+                        pl.semaphore_wait(turn, 1)
+
+                    send_sk(m).start()
+
+        @pl.when(kind == 1)
+        def _():
+            @pl.when((s == 3) & (m == 0))
+            def _():
+                up_load.wait()
+
+            @pl.when(s == 0)
+            def _():
+                send_dk(m).wait_recv()
+
+                @pl.when(m == 1)
+                def _():
+                    product(2, dk)
+                    begin(2)
+
+            @pl.when(s < 3)
+            def _():
+                send_up(m).wait_recv()
+
+            @pl.when(s == 1)
+            def _():
+                send_dk(m).wait_recv()
+
+            @pl.when(s < 2)
+            def _():
+                for n in columns:
+                    tot[rows, n] = (
+                        up[rows, n].astype(F32)
+                        + lax.dot_general(dk[rows, :], w3[n, :], NT, preferred_element_type=F32)
+                    ).astype(BF16)
+
+            @pl.when(s >= 2)
+            def _():
+                tot[rows, :] = up[rows, :]
+
+            for n in columns:
+                dpre[rows, n] = (
+                    lax.dot_general(tot[rows, :], w2[n, :], NT, preferred_element_type=F32)
+                    * pre[rows, n]
+                ).astype(BF16)
+
+            @pl.when(s == 2)
+            def _():
+                for n in columns:
+                    dk[rows, n] = lax.dot_general(
+                        dpre[rows, :], w3[n, :], NT, preferred_element_type=F32
+                    ).astype(BF16)
+                send_dk(m).start()
+
+            for n in columns:
+                gi[rows, n] = (
+                    tot[rows, n].astype(F32)
+                    + lax.dot_general(dpre[rows, :], w1[n, :], NT, preferred_element_type=F32)
+                ).astype(BF16)
+
+            @pl.when(s > 0)
+            def _():
+                send_up(m).start()
+
+            @pl.when(s == 3)
+            def _():
+                for n in columns:
+                    dk[rows, n] = lax.dot_general(
+                        dpre[rows, :], w3[n, :], NT, preferred_element_type=F32
+                    ).astype(BF16)
+                send_dk(m).start()
+
+        @pl.when(kind == on3)
+        def _():
+            for n in columns:
+                lt[0, n, rows] = x[rows, n].T
+                lt[1, n, rows] = gat[rows, n].T
+
+            @pl.when(s < 2)
+            def _():
+                for n in columns:
+                    lt[2, n, rows] = po[rows, n].T
+
+            @pl.when(s >= 2)
+            def _():
+                for n in columns:
+                    lt[2, n, rows] = sk[rows, n].T
+
+    @pl.when(s == 1)
+    def _():
+        product(2, dk)
+        begin(2)
+
+    @pl.when(s >= 2)
+    def _():
+        product(2, dpre)
+        begin(2)
+
+    product(1, tot)
+    begin(1)
+    product(0, dpre)
+    begin(0)
+    order = BLOCKS[::-1]
     for block in order:
         k, _, col, width, colour, by = block
         cols = pl.ds(col, width)
@@ -313,9 +360,9 @@
         )
         xs[k, 0, :, cols] = part[:40].astype(BF16)
         xs[k, 1, :, cols] = part[40:].astype(BF16)
-        if last == 3:
+        if last == 0:
             pair(k).start()
-    for k in (1, 2, 0):
+    for k in (2, 1, 0):
         pair(k).wait_recv()
         (g_in, g_out, g_skip)[k][...] = xs[k, xh].astype(F32) + xr[k].astype(F32)
     for block in order:
@@ -326,11 +373,11 @@
         pair(k).wait_send()
     for m in range(2):
 
-        @pl.when(s < 3)
+        @pl.when((s == 0) | (s == 2))
         def _():
             send_x(m).wait_send()
 
-        @pl.when(s < 2)
+        @pl.when(s == 0)
         def _():
             send_sk(m).wait_send()
 
@@ -341,13 +388,21 @@
         @pl.when(s >= 2)
         def _():
             send_dk(m).wait_send()
+
+
+def deliver(*refs):
+    sem = refs[-1]
+    copies = [pltpu.make_async_copy(refs[n], refs[5 + n], sem.at[n]) for n in range(5)]
+    for copy in copies:
+        copy.start()
+    for copy in copies:
+        copy.wait()
 
 
 def body(latents, cotangent, timesteps, time_table, w_in, w_out, w_skip):
     rows = 2 * R
-    bias = time_table[0][timesteps[:, 0]].astype(F32)[:, None, :]
     vmem = pl.BlockSpec(memory_space=pltpu.VMEM)
-    hbm = pl.BlockSpec(memory_space=pl.ANY)
+    hbm = pl.BlockSpec(memory_space=pltpu.HBM)
     act = pltpu.VMEM((rows, C), BF16)
     weight = pltpu.VMEM((C, C), BF16)
     quarter = pltpu.VMEM((3, 4, 80, C), BF16)
@@ -355,14 +410,16 @@
     dma = pltpu.SemaphoreType.DMA
     out_act = jax.ShapeDtypeStruct((rows, C), BF16)
     out_grad = jax.ShapeDtypeStruct((40, C), F32)
-    po, gi, g_in, g_out, g_skip = pl.pallas_call(
+    outs = (out_act, out_act, out_grad, out_grad, out_grad)
+    results = pl.pallas_call(
         kernel,
         name="window",
-        out_shape=(out_act, out_act, out_grad, out_grad, out_grad),
-        in_specs=[hbm, hbm, vmem, hbm, hbm, hbm],
+        out_shape=outs,
+        in_specs=[vmem, vmem, pl.BlockSpec(memory_space=pltpu.SMEM), vmem, hbm, hbm, hbm],
         out_specs=[vmem] * 5,
         scratch_shapes=[
             weight, weight, weight,
+            pltpu.VMEM((2, 1, C), F32),
             act, act, act, act,
             pltpu.VMEM((rows, C), F32),
             act, act, act,
@@ -373,6 +430,7 @@
             pltpu.VMEM((3, 2, 40, C), BF16),
             pltpu.VMEM((3, 40, C), BF16),
             dma((3,)),
+            pltpu.SemaphoreType.REGULAR,
             dma((2,)), dma((3,)),
             dma((2,)), dma((2,)),
             dma((2,)), dma((3,)),
@@ -381,12 +439,21 @@
             dma((3,)), dma((3,)),
         ],
         compiler_params=pltpu.CompilerParams(
-            collective_id=0, has_side_effects=True, vmem_limit_bytes=60 * 1024 * 1024
+            collective_id=0, has_side_effects=True, vmem_limit_bytes=50_000_000
         ),
     )(
-        latents.reshape(rows, C), cotangent.reshape(rows, C), bias,
+        latents.reshape(rows, C), cotangent.reshape(rows, C), timesteps, time_table.reshape(1000, C),
         w_in.reshape(C, C), w_out.reshape(C, C), w_skip.reshape(C, C),
     )
+    po, gi, g_in, g_out, g_skip = pl.pallas_call(
+        deliver,
+        name="deliver",
+        out_shape=outs,
+        in_specs=[vmem] * 5,
+        out_specs=[hbm] * 5,
+        scratch_shapes=[dma((5,))],
+        compiler_params=pltpu.CompilerParams(vmem_limit_bytes=4_000_000),
+    )(*results)
     return (
         po.reshape(1, 2, R, C),
         gi.reshape(1, 2, R, C),

time: 138 us -> 126 us (0.913)
  Pallas kernels: 126 us -> 119 us
  local copies, waits for them, and re-layouts: 10.8 us -> 4.64 us
    pallas_call x1 -> x2, Pallas kernels: 126 us -> 119 us  [the longest x1 118 us: body(): pl.pallas_call(kernel, name='window', out_shape=outs, in_specs=[vmem, vme...]
    unnamed x9 -> x7, local copies, waits for them, and re-layouts: 9.62 us -> 4.64 us
where the time goes in v2:
time: 126 us; the launch traced here: 125 us
  Pallas kernels  119 us (94%)
  local copies, waits for them, and re-layouts  4.64 us (4%)
    pallas_call x1, Pallas kernels, body(): pl.pallas_call(kernel, name='window', out_shape=outs, in_specs=[vmem, vme...  118 us
    unnamed x7, local copies, waits for them, and re-layouts  4.64 us

profile of v2, /device:TPU:0, one launch (start us, length us, event | category | flops | bytes accessed | tf_op | source)
XLA Modules:
  0.0 124.7 jit_solution(13151058097321304698)
XLA Ops:
  0.6 0.7 copy.12.steps
  1.4 0.0 copy-start
  1.4 1.7 %copy-done = bf16[1,1000,1280]{2,1,0:T(8,128)(2,1)S(1)} copy-done((bf16[1,1000,1280]{2,1,0:T(8,128)(2,1)S(1)}, bf16[1,1000,1280]{2,1,0:T(8,128)(2,1)}, u32[]{:S(2)}) %copy-start) | copy-done | bytes 2560024
  3.1 0.0 copy-start.1
  3.1 1.1 copy-done.1
  4.2 0.0 copy-start.2
  4.2 1.1 copy-done.2
  5.3 118.2 %window.1 = (bf16[256,1280]{1,0:T(8,128)(2,1)S(1)}, bf16[256,1280]{1,0:T(8,128)(2,1)S(1)}, f32[40,1280]{1,0:T(8,128)S(1)}, f32[40,1280]{1,0:T(8,128)S(1)}, f32[40,1280]{1,0:T(8,128)S(1)}) custom-call(bf16[256,1280]{1,0:T(8,128)(2,1)S(1)} %bitcast.12, bf16[256,1280]{1,0:T(8,128)(2,1)S(1)} %bitcast.13, s32[2,1]{1,0:T(2,128)S(1)} %copy.12.steps, ...), custom_call_target="tpu_custom_call" | custom-call | tf_op jit(solution)/shard_map/window/pallas_call | solution.py:414
  123.4 1.3 %deliver.1 = (bf16[256,1280]{1,0:T(8,128)(2,1)}, bf16[256,1280]{1,0:T(8,128)(2,1)}, f32[40,1280]{1,0:T(8,128)}, f32[40,1280]{1,0:T(8,128)}, f32[40,1280]{1,0:T(8,128)}) custom-call(bf16[256,1280]{1,0:T(8,128)(2,1)S(1)} %get-tuple-element.15.refs_0_, bf16[256,1280]{1,0:T(8,128)(2,1)S(1)} %get-tuple-element.16.refs_1_, ...), custom_call_target="tpu_custom_call" | custom-call | tf_op jit(solution)/shard_map/deliver/pallas_call | solution.py:448
Async XLA Ops:
  1.4 1.7 %copy-start = (bf16[1,1000,1280]{2,1,0:T(8,128)(2,1)S(1)}, bf16[1,1000,1280]{2,1,0:T(8,128)(2,1)}, u32[]{:S(2)}) copy-start(bf16[1,1000,1280]{2,1,0:T(8,128)(2,1)} %param.10) | copy-start | bytes 7680004
  3.1 1.1 copy-start.1
  4.2 1.1 copy-start.2

commit v3 on v2

--- a/solution.py
+++ b/solution.py
@@ -12,19 +12,17 @@
 R = 128
 TILE = 256
 NT = (((1,), (1,)), ((), ()))
-SPLITS = (
-    ((0, 384, 0, 1), (384, 256, 0, -1), (640, 256, 1, 1), (896, 384, 1, -1)),
-    ((0, 256, 0, 1), (256, 384, 0, -1), (640, 384, 1, 1), (1024, 256, 1, -1)),
-    ((0, 384, 0, 1), (384, 256, 0, -1), (640, 256, 1, 1), (896, 384, 1, -1)),
-)
-BLOCKS = tuple((k, n, *block) for k in range(3) for n, block in enumerate(SPLITS[k]))
+BLOCKS = ((0, 0, 384, 0, 1), (1, 384, 256, 0, -1), (2, 640, 256, 1, 1), (3, 896, 384, 1, -1))
+Q = C // 4
 
 
 def kernel(
     lat, cot, steps, table, w_in, w_out, w_skip,
     po, gi, g_in, g_out, g_skip,
     w1, w2, w3, bias, x, up, sk, dk, pre, gat, tot, dpre, lt, grads, r1, r2, r3, s1, q1, q2, q3, xs, xr,
+    left, stage, right, part, p1, p2, p3, hs, hr, fs, fr,
     wsem, turn, x_s, x_r, sk_s, sk_r, up_s, up_r, dk_s, dk_r, rs_s, rs_r, xh_s, xh_r,
+    ag_s, ag_r, fw_s, fw_r, aa_s, aa_r, js_s, js_r, fin_s, fin_r,
 ):
     s = lax.axis_index("segment")
     dp = lax.axis_index("dp")
@@ -59,7 +57,7 @@
     barrier = pltpu.get_barrier_semaphore()
     for by in (1, 2, 3):
         pl.semaphore_signal(barrier, inc=1, device_id={"segment": (s + by) % 4}, device_id_type=MESH)
-    for other in (along(0, 1), along(0, -1), along(1, 1), along(1, -1), partner):
+    for other in [along(axis, by) for axis in (0, 1) for by in (1, 2, 3)] + [partner]:
         pl.semaphore_signal(barrier, inc=1, device_id={"dp": other}, device_id_type=MESH)
     row = lax.broadcasted_iota(jnp.int32, (8, table.shape[0]), 0)
     chosen = jnp.where(row == 0, steps[0, 0], steps[1, 0])
@@ -67,7 +65,7 @@
     found = jnp.dot(hot.astype(F32).astype(BF16), table[...], preferred_element_type=F32)
     bias[0] = found[0:1]
     bias[1] = found[1:2]
-    pl.semaphore_wait(barrier, 8)
+    pl.semaphore_wait(barrier, 10)
 
     def hand(buf, dst, m, send, recv, to):
         rows = pl.ds(pl.multiple_of(m * R, R), R)
@@ -91,54 +89,137 @@
     columns = [pl.ds(n * TILE, TILE) for n in range(C // TILE)]
     on3 = s // 3
 
-    def ring(stage, msg, block, src, dst, axis, by):
-        n = block[0] * 4 + block[1]
+    here = (z, y)
+
+    def ring(step, msg, block, src, dst, axis, by):
+        n = block[0]
         return pltpu.make_async_remote_copy(
-            src_ref=src, dst_ref=dst, send_sem=rs_s.at[stage, msg, n], recv_sem=rs_r.at[stage, msg, n],
+            src_ref=src, dst_ref=dst, send_sem=rs_s.at[step, msg, n], recv_sem=rs_r.at[step, msg, n],
             device_id={"dp": along(axis, by)}, device_id_type=MESH,
         )
 
     def piece(block, pos):
-        k, _, col, width, colour, _ = block
+        _, col, width, colour, _ = block
         cols = pl.ds(col, width)
         if colour == 0:
-            return grads.at[k, pos % 4, :, :, cols]
-        return grads.at[k, :, pos % 4, :, cols]
+            return grads.at[pos % 4, :, :, cols]
+        return grads.at[:, pos % 4, :, cols]
 
     def first(block, msg):
-        k, _, col, width, colour, by = block
+        _, col, width, colour, by = block
         cols = pl.ds(col, width)
-        pos = (z, y)[colour]
+        pos = here[colour]
         if msg == 0:
-            return ring(0, 0, block, piece(block, pos + 2), r1.at[k, :, :, cols], colour, by)
+            return ring(0, 0, block, piece(block, pos + 2), r1.at[:, :, cols], colour, by)
         if msg == 1:
-            return ring(0, 1, block, r1.at[k, :, :, cols], r2.at[k, :, :, cols], colour, by)
-        return ring(0, 2, block, piece(block, pos - by + 4), r3.at[k, :, :, cols], colour, -by)
+            return ring(0, 1, block, r1.at[:, :, cols], r2.at[:, :, cols], colour, by)
+        return ring(0, 2, block, piece(block, pos - by + 4), r3.at[:, :, cols], colour, -by)
 
     def second(block, msg):
-        k, _, col, width, colour, by = block
+        _, col, width, colour, by = block
         cols = pl.ds(col, width)
-        pos = (y, z)[colour]
         axis = 1 - colour
+        pos = here[axis]
         if msg == 0:
-            return ring(1, 0, block, s1.at[k, (pos + 2) % 4, :, cols], q1.at[k, :, cols], axis, by)
+            return ring(1, 0, block, s1.at[(pos + 2) % 4, :, cols], q1.at[:, cols], axis, by)
         if msg == 1:
-            return ring(1, 1, block, q1.at[k, :, cols], q2.at[k, :, cols], axis, by)
-        return ring(1, 2, block, s1.at[k, (pos - by + 4) % 4, :, cols], q3.at[k, :, cols], axis, -by)
-
-    def product(k, right):
+            return ring(1, 1, block, q1.at[:, cols], q2.at[:, cols], axis, by)
+        return ring(1, 2, block, s1.at[(pos - by + 4) % 4, :, cols], q3.at[:, cols], axis, -by)
+
+    def product(other):
         @pl.loop(0, 4)
         def _(zp):
-            left = lt[k, pl.ds(pl.multiple_of(zp * 320, 320), 320), :]
+            mine = lt[pl.ds(pl.multiple_of(zp * 320, 320), 320), :]
             for n in columns:
-                acc = jnp.dot(left, right[:, n], preferred_element_type=F32).astype(BF16)
+                acc = jnp.dot(mine, other[:, n], preferred_element_type=F32).astype(BF16)
                 for yp in range(4):
-                    grads[k, zp, yp, :, n] = acc[yp * 80 : (yp + 1) * 80]
-
-    def begin(k):
-        for block in BLOCKS[4 * k : 4 * k + 4]:
+                    grads[zp, yp, :, n] = acc[yp * 80 : (yp + 1) * 80]
+
+        for block in BLOCKS:
             first(block, 0).start()
             first(block, 2).start()
+
+    def remote(src, dst, send, recv, axis, by):
+        return pltpu.make_async_remote_copy(
+            src_ref=src, dst_ref=dst, send_sem=send, recv_sem=recv,
+            device_id={"dp": along(axis, by)}, device_id_type=MESH,
+        )
+
+    def slot(job, m, by=0):
+        return pl.ds(pl.multiple_of(((here[job] + by + 4) % 4 * 2 + m) * R, R), R)
+
+    def spread(job, m, d):
+        ref = left.at[job, :, slot(job, m)]
+        return remote(ref, ref, ag_s.at[job, m, d], ag_r.at[job, m, d], job, 1 - 2 * d)
+
+    def relay(job, m, d):
+        by = 1 - 2 * d
+        ref = left.at[job, pl.ds(d * 640, 640), slot(job, m, -by)]
+        return remote(ref, ref, fw_s.at[job, m, d], fw_r.at[job, m, d], job, by)
+
+    def forward(m):
+        for job in range(2):
+            for d in range(2):
+                spread(job, m, d).wait_recv()
+                relay(job, m, d).start()
+
+    def turned(job, m, by):
+        rows = pl.ds(pl.multiple_of(m * R, R), R)
+        return remote(
+            stage.at[job, (here[job] + by) % 4, rows], right.at[job, slot(job, m)],
+            aa_s.at[job, m, by - 1], aa_r.at[job, m, by - 1], job, by,
+        )
+
+    def swap(job, m):
+        rows = pl.ds(pl.multiple_of(m * R, R), R)
+        value = (dpre, tot)[job]
+        for q in range(4):
+            stage[job, q, rows, :] = value[rows, q * Q : (q + 1) * Q]
+        for by in (1, 3, 2):
+            turned(job, m, by).start()
+        right[job, slot(job, m), :] = stage[job, here[job], rows, :]
+
+    def sums(job, half, msg):
+        by = 1 - 2 * half
+        axis = 1 - job
+        pos = here[axis]
+        o = pl.ds(2 * half, 2)
+        sems = (js_s.at[job, half, msg], js_r.at[job, half, msg])
+        if msg == 0:
+            return remote(part.at[job, o, (pos + 2) % 4], p1.at[job, o], *sems, axis, by)
+        if msg == 1:
+            return remote(p1.at[job, o], p2.at[job, o], *sems, axis, by)
+        return remote(part.at[job, o, (pos - by + 4) % 4], p3.at[job, o], *sems, axis, -by)
+
+    def block_product(job):
+        @pl.loop(0, 4)
+        def _(zp):
+            acc = jnp.dot(
+                left[job, pl.ds(pl.multiple_of(zp * 320, 320), 320), :], right[job],
+                preferred_element_type=F32,
+            ).astype(BF16)
+            for yp in range(4):
+                if job == 0:
+                    part[0, zp, yp] = acc[yp * 80 : (yp + 1) * 80]
+                else:
+                    part[1, yp, zp] = acc[yp * 80 : (yp + 1) * 80]
+
+        for half in range(2):
+            sums(job, half, 0).start()
+            sums(job, half, 2).start()
+
+    def pair(k):
+        src, dst = ((hs.at[0, 1 - xh], hr.at[0]), (hs.at[1, 1 - xh], hr.at[1]), (xs.at[1 - xh], xr))[k]
+        return pltpu.make_async_remote_copy(
+            src_ref=src, dst_ref=dst, send_sem=xh_s.at[k], recv_sem=xh_r.at[k],
+            device_id={"dp": partner}, device_id_type=MESH,
+        )
+
+    def last(job, by):
+        return remote(
+            fs.at[job, (here[job] + by) % 4], fr.at[job, here[job]],
+            fin_s.at[job, by - 1], fin_r.at[job, by - 1], job, by,
+        )
 
     @pl.loop(0, 4)
     def _(i):
@@ -227,8 +308,7 @@
 
                 @pl.when(m == 1)
                 def _():
-                    product(2, dk)
-                    begin(2)
+                    product(dk)
 
             @pl.when(s < 3)
             def _():
@@ -256,6 +336,11 @@
                     * pre[rows, n]
                 ).astype(BF16)
 
+            @pl.when(s == 0)
+            def _():
+                swap(1, m)
+                swap(0, m)
+
             @pl.when(s == 2)
             def _():
                 for n in columns:
@@ -282,95 +367,147 @@
                     ).astype(BF16)
                 send_dk(m).start()
 
+            @pl.when(s > 0)
+            def _():
+                swap(1, m)
+                swap(0, m)
+
         @pl.when(kind == on3)
         def _():
             for n in columns:
-                lt[0, n, rows] = x[rows, n].T
-                lt[1, n, rows] = gat[rows, n].T
+                left[0, n, slot(0, m)] = x[rows, n].T
+                left[1, n, slot(1, m)] = gat[rows, n].T
+            for job in range(2):
+                for d in range(2):
+                    spread(job, m, d).start()
 
             @pl.when(s < 2)
             def _():
                 for n in columns:
-                    lt[2, n, rows] = po[rows, n].T
+                    lt[n, rows] = po[rows, n].T
 
             @pl.when(s >= 2)
             def _():
                 for n in columns:
-                    lt[2, n, rows] = sk[rows, n].T
+                    lt[n, rows] = sk[rows, n].T
+
+        @pl.when((i >= 1 + 2 * on3) & (i <= 2 + on3))
+        def _():
+            forward(i - 1 - 2 * on3)
+
+    @pl.when(s == 3)
+    def _():
+        forward(1)
 
     @pl.when(s == 1)
     def _():
-        product(2, dk)
-        begin(2)
+        product(dk)
 
     @pl.when(s >= 2)
     def _():
-        product(2, dpre)
-        begin(2)
-
-    product(1, tot)
-    begin(1)
-    product(0, dpre)
-    begin(0)
-    order = BLOCKS[::-1]
-    for block in order:
-        k, _, col, width, colour, by = block
+        product(dpre)
+
+    def gathered(job):
+        for m in range(2):
+            for d in range(2):
+                relay(job, m, d).wait_recv()
+            for by in (1, 2, 3):
+                turned(job, m, by).wait_recv()
+
+    gathered(1)
+    block_product(1)
+    for block in BLOCKS:
+        _, col, width, colour, by = block
         cols = pl.ds(col, width)
         first(block, 0).wait_recv()
-        pos = (z, y)[colour] + by + 4
-        r1[k, :, :, cols] = (
-            r1[k, :, :, cols].astype(F32) + piece(block, pos)[...].astype(F32)
+        r1[:, :, cols] = (
+            r1[:, :, cols].astype(F32) + piece(block, here[colour] + by + 4)[...].astype(F32)
         ).astype(BF16)
         first(block, 1).start()
-    for block in order:
-        k, _, col, width, colour, by = block
+    gathered(0)
+    block_product(0)
+    for job in (1, 0):
+        for half in range(2):
+            o = pl.ds(2 * half, 2)
+            sums(job, half, 0).wait_recv()
+            pos = (here[1 - job] + 5 - 2 * half) % 4
+            p1[job, o] = (p1[job, o].astype(F32) + part[job, o, pos].astype(F32)).astype(BF16)
+            sums(job, half, 1).start()
+    for block in BLOCKS:
+        _, col, width, colour, by = block
         cols = pl.ds(col, width)
         first(block, 1).wait_recv()
         first(block, 2).wait_recv()
-        s1[k, :, :, cols] = (
-            piece(block, (z, y)[colour])[...].astype(F32)
-            + r2[k, :, :, cols].astype(F32)
-            + r3[k, :, :, cols].astype(F32)
+        s1[:, :, cols] = (
+            piece(block, here[colour])[...].astype(F32)
+            + r2[:, :, cols].astype(F32)
+            + r3[:, :, cols].astype(F32)
         ).astype(BF16)
         second(block, 0).start()
         second(block, 2).start()
-    for block in order:
-        k, _, col, width, colour, by = block
+    for job in (1, 0):
+        for half in range(2):
+            sums(job, half, 1).wait_recv()
+            sums(job, half, 2).wait_recv()
+            for o in (2 * half, 2 * half + 1):
+                total = (
+                    part[job, o, here[1 - job]].astype(F32)
+                    + p2[job, o].astype(F32)
+                    + p3[job, o].astype(F32)
+                )
+                hs[job, 0, o] = total[:40].astype(BF16)
+                hs[job, 1, o] = total[40:].astype(BF16)
+        pair(job).start()
+    for block in BLOCKS:
+        _, col, width, colour, by = block
         cols = pl.ds(col, width)
         second(block, 0).wait_recv()
-        pos = ((y, z)[colour] + by + 4) % 4
-        q1[k, :, cols] = (q1[k, :, cols].astype(F32) + s1[k, pos, :, cols].astype(F32)).astype(BF16)
+        pos = (here[1 - colour] + by + 4) % 4
+        q1[:, cols] = (q1[:, cols].astype(F32) + s1[pos, :, cols].astype(F32)).astype(BF16)
         second(block, 1).start()
-
-    def pair(k):
-        return pltpu.make_async_remote_copy(
-            src_ref=xs.at[k, 1 - xh], dst_ref=xr.at[k], send_sem=xh_s.at[k], recv_sem=xh_r.at[k],
-            device_id={"dp": partner}, device_id_type=MESH,
-        )
-
-    for block in order:
-        k, last, col, width, colour, by = block
+    for job in (1, 0):
+        pair(job).wait_recv()
+        for o in range(4):
+            fs[job, o] = (hs[job, xh, o].astype(F32) + hr[job, o].astype(F32)).astype(BF16)
+        for by in (1, 3, 2):
+            last(job, by).start()
+        fr[job, here[job]] = fs[job, here[job]]
+    for block in BLOCKS:
+        _, col, width, colour, by = block
         cols = pl.ds(col, width)
         second(block, 1).wait_recv()
         second(block, 2).wait_recv()
-        part = (
-            s1[k, (y, z)[colour], :, cols].astype(F32)
-            + q2[k, :, cols].astype(F32)
-            + q3[k, :, cols].astype(F32)
+        total = (
+            s1[here[1 - colour], :, cols].astype(F32)
+            + q2[:, cols].astype(F32)
+            + q3[:, cols].astype(F32)
         )
-        xs[k, 0, :, cols] = part[:40].astype(BF16)
-        xs[k, 1, :, cols] = part[40:].astype(BF16)
-        if last == 0:
-            pair(k).start()
-    for k in (2, 1, 0):
-        pair(k).wait_recv()
-        (g_in, g_out, g_skip)[k][...] = xs[k, xh].astype(F32) + xr[k].astype(F32)
-    for block in order:
+        xs[0, :, cols] = total[:40].astype(BF16)
+        xs[1, :, cols] = total[40:].astype(BF16)
+    pair(2).start()
+    for job in (1, 0):
+        for by in (1, 2, 3):
+            last(job, by).wait_recv()
+        for q in range(4):
+            (g_in, g_out)[job][:, q * Q : (q + 1) * Q] = fr[job, q].astype(F32)
+    pair(2).wait_recv()
+    g_skip[...] = xs[xh].astype(F32) + xr[...].astype(F32)
+    for block in BLOCKS:
         for msg in range(3):
             first(block, msg).wait_send()
             second(block, msg).wait_send()
     for k in range(3):
         pair(k).wait_send()
+    for job in range(2):
+        for n in range(3):
+            last(job, n + 1).wait_send()
+            for m in range(2):
+                turned(job, m, n + 1).wait_send()
+                sums(job, m, n).wait_send()
+        for m in range(2):
+            for d in range(2):
+                spread(job, m, d).wait_send()
+                relay(job, m, d).wait_send()
     for m in range(2):
 
         @pl.when((s == 0) | (s == 2))
@@ -405,8 +542,10 @@
     hbm = pl.BlockSpec(memory_space=pltpu.HBM)
     act = pltpu.VMEM((rows, C), BF16)
     weight = pltpu.VMEM((C, C), BF16)
-    quarter = pltpu.VMEM((3, 4, 80, C), BF16)
-    sixteenth = pltpu.VMEM((3, 80, C), BF16)
+    quarter = pltpu.VMEM((4, 80, C), BF16)
+    sixteenth = pltpu.VMEM((80, C), BF16)
+    sums = pltpu.VMEM((2, 4, 80, Q), BF16)
+    halves = pltpu.VMEM((2, 4, 40, Q), BF16)
     dma = pltpu.SemaphoreType.DMA
     out_act = jax.ShapeDtypeStruct((rows, C), BF16)
     out_grad = jax.ShapeDtypeStruct((40, C), F32)
@@ -423,20 +562,32 @@
             act, act, act, act,
             pltpu.VMEM((rows, C), F32),
             act, act, act,
-            pltpu.VMEM((3, C, rows), BF16),
-            pltpu.VMEM((3, 4, 4, 80, C), BF16),
+            pltpu.VMEM((C, rows), BF16),
+            pltpu.VMEM((4, 4, 80, C), BF16),
             quarter, quarter, quarter, quarter,
             sixteenth, sixteenth, sixteenth,
-            pltpu.VMEM((3, 2, 40, C), BF16),
-            pltpu.VMEM((3, 40, C), BF16),
+            pltpu.VMEM((2, 40, C), BF16),
+            pltpu.VMEM((40, C), BF16),
+            pltpu.VMEM((2, C, 4 * rows), BF16),
+            pltpu.VMEM((2, 4, rows, Q), BF16),
+            pltpu.VMEM((2, 4 * rows, Q), BF16),
+            pltpu.VMEM((2, 4, 4, 80, Q), BF16),
+            sums, sums, sums,
+            pltpu.VMEM((2, 2, 4, 40, Q), BF16),
+            halves, halves, halves,
             dma((3,)),
             pltpu.SemaphoreType.REGULAR,
             dma((2,)), dma((3,)),
             dma((2,)), dma((2,)),
             dma((2,)), dma((3,)),
             dma((2,)), dma((2,)),
-            dma((2, 3, 12)), dma((2, 3, 12)),
+            dma((2, 3, 4)), dma((2, 3, 4)),
             dma((3,)), dma((3,)),
+            dma((2, 2, 2)), dma((2, 2, 2)),
+            dma((2, 2, 2)), dma((2, 2, 2)),
+            dma((2, 2, 3)), dma((2, 2, 3)),
+            dma((2, 2, 3)), dma((2, 2, 3)),
+            dma((2, 3)), dma((2, 3)),
         ],
         compiler_params=pltpu.CompilerParams(
             collective_id=0, has_side_effects=True, vmem_limit_bytes=50_000_000

time: 126 us -> 111 us (0.88)
  Pallas kernels: 119 us -> 105 us
    pallas_call x1, Pallas kernels: 118 us -> 104 us  [body(): pl.pallas_call(kernel, name='window', out_shape=outs, in_specs=[vmem, vme...]
where the time goes in v3:
time: 111 us; the launch traced here: 110 us
  Pallas kernels  105 us (95%)
  local copies, waits for them, and re-layouts  4.64 us (4%)
    pallas_call x1, Pallas kernels, body(): pl.pallas_call(kernel, name='window', out_shape=outs, in_specs=[vmem, vme...  104 us
    unnamed x7, local copies, waits for them, and re-layouts  4.64 us

profile of v3, /device:TPU:0, one launch (start us, length us, event | category | flops | bytes accessed | tf_op | source)
XLA Modules:
  0.0 110.4 jit_solution(18280398004122939857)
XLA Ops:
  0.6 0.7 copy.12.steps
  1.4 0.0 copy-start
  1.4 1.7 %copy-done = bf16[1,1000,1280]{2,1,0:T(8,128)(2,1)S(1)} copy-done((bf16[1,1000,1280]{2,1,0:T(8,128)(2,1)S(1)}, bf16[1,1000,1280]{2,1,0:T(8,128)(2,1)}, u32[]{:S(2)}) %copy-start) | copy-done | bytes 2560024
  3.1 0.0 copy-start.1
  3.1 1.1 copy-done.1
  4.2 0.0 copy-start.2
  4.2 1.1 copy-done.2
  5.3 103.8 %window.1 = (bf16[256,1280]{1,0:T(8,128)(2,1)S(1)}, bf16[256,1280]{1,0:T(8,128)(2,1)S(1)}, f32[40,1280]{1,0:T(8,128)S(1)}, f32[40,1280]{1,0:T(8,128)S(1)}, f32[40,1280]{1,0:T(8,128)S(1)}) custom-call(bf16[256,1280]{1,0:T(8,128)(2,1)S(1)} %bitcast.12, bf16[256,1280]{1,0:T(8,128)(2,1)S(1)} %bitcast.13, s32[2,1]{1,0:T(2,128)S(1)} %copy.12.steps, ...), custom_call_target="tpu_custom_call" | custom-call | tf_op jit(solution)/shard_map/window/pallas_call | solution.py:553
  109.1 1.3 %deliver.1 = (bf16[256,1280]{1,0:T(8,128)(2,1)}, bf16[256,1280]{1,0:T(8,128)(2,1)}, f32[40,1280]{1,0:T(8,128)}, f32[40,1280]{1,0:T(8,128)}, f32[40,1280]{1,0:T(8,128)}) custom-call(bf16[256,1280]{1,0:T(8,128)(2,1)S(1)} %get-tuple-element.15.refs_0_, bf16[256,1280]{1,0:T(8,128)(2,1)S(1)} %get-tuple-element.16.refs_1_, ...), custom_call_target="tpu_custom_call" | custom-call | tf_op jit(solution)/shard_map/deliver/pallas_call | solution.py:599
Async XLA Ops:
  1.4 1.7 %copy-start = (bf16[1,1000,1280]{2,1,0:T(8,128)(2,1)S(1)}, bf16[1,1000,1280]{2,1,0:T(8,128)(2,1)}, u32[]{:S(2)}) copy-start(bf16[1,1000,1280]{2,1,0:T(8,128)(2,1)} %param.10) | copy-start | bytes 7680004
  3.1 1.1 copy-start.1
  4.2 1.1 copy-start.2

commit v4 on v3

--- a/solution.py
+++ b/solution.py
@@ -19,7 +19,7 @@
 def kernel(
     lat, cot, steps, table, w_in, w_out, w_skip,
     po, gi, g_in, g_out, g_skip,
-    w1, w2, w3, bias, x, up, sk, dk, pre, gat, tot, dpre, lt, grads, r1, r2, r3, s1, q1, q2, q3, xs, xr,
+    w1, w2, w3, rows_t, bias, acc, x, up, sk, dk, pre, gat, tot, dpre, lt, grads, r1, r2, r3, s1, q1, q2, q3, xs, xr,
     left, stage, right, part, p1, p2, p3, hs, hr, fs, fr,
     wsem, turn, x_s, x_r, sk_s, sk_r, up_s, up_r, dk_s, dk_r, rs_s, rs_r, xh_s, xh_r,
     ag_s, ag_r, fw_s, fw_r, aa_s, aa_r, js_s, js_r, fin_s, fin_r,
@@ -38,7 +38,7 @@
     partner = z * 8 + y * 2 + (1 - xh)
     loads = [
         pltpu.make_async_copy(src, dst, wsem.at[n])
-        for n, (src, dst) in enumerate(((w_in, w1), (w_out, w2), (w_skip, w3)))
+        for n, (src, dst) in enumerate(((w_in, w1), (table, rows_t), (w_out, w2), (w_skip, w3)))
     ]
     x_load = pltpu.make_async_copy(lat, x, x_r.at[2])
     up_load = pltpu.make_async_copy(cot, up, up_r.at[2])
@@ -59,13 +59,6 @@
         pl.semaphore_signal(barrier, inc=1, device_id={"segment": (s + by) % 4}, device_id_type=MESH)
     for other in [along(axis, by) for axis in (0, 1) for by in (1, 2, 3)] + [partner]:
         pl.semaphore_signal(barrier, inc=1, device_id={"dp": other}, device_id_type=MESH)
-    row = lax.broadcasted_iota(jnp.int32, (8, table.shape[0]), 0)
-    chosen = jnp.where(row == 0, steps[0, 0], steps[1, 0])
-    hot = lax.broadcasted_iota(jnp.int32, (8, table.shape[0]), 1) == chosen
-    found = jnp.dot(hot.astype(F32).astype(BF16), table[...], preferred_element_type=F32)
-    bias[0] = found[0:1]
-    bias[1] = found[1:2]
-    pl.semaphore_wait(barrier, 10)
 
     def hand(buf, dst, m, send, recv, to):
         rows = pl.ds(pl.multiple_of(m * R, R), R)
@@ -247,7 +240,14 @@
             @pl.when(i == 0)
             def _():
                 loads[1].wait()
+                row = lax.broadcasted_iota(jnp.int32, (8, table.shape[0]), 0)
+                chosen = jnp.where(row == 0, steps[0], steps[1])
+                hot = lax.broadcasted_iota(jnp.int32, (8, table.shape[0]), 1) == chosen
+                found = jnp.dot(hot.astype(F32).astype(BF16), rows_t[...], preferred_element_type=F32)
+                bias[0] = found[0:1]
+                bias[1] = found[1:2]
                 loads[2].wait()
+                loads[3].wait()
 
             @pl.when(s >= 2)
             def _():
@@ -266,6 +266,10 @@
                     + jnp.dot(gat[rows, :], w2[:, n], preferred_element_type=F32)
                 ).astype(BF16)
 
+            @pl.when(i == 0)
+            def _():
+                pl.semaphore_wait(barrier, 10)
+
             @pl.when(s < 3)
             def _():
                 send_x(m).start()
@@ -302,9 +306,13 @@
             def _():
                 up_load.wait()
 
-            @pl.when(s == 0)
+            @pl.when(s < 2)
             def _():
                 send_dk(m).wait_recv()
+                for n in columns:
+                    acc[:, n] = lax.dot_general(
+                        dk[rows, :], w3[n, :], NT, preferred_element_type=F32
+                    )
 
                 @pl.when(m == 1)
                 def _():
@@ -314,17 +322,9 @@
             def _():
                 send_up(m).wait_recv()
 
-            @pl.when(s == 1)
-            def _():
-                send_dk(m).wait_recv()
-
             @pl.when(s < 2)
             def _():
-                for n in columns:
-                    tot[rows, n] = (
-                        up[rows, n].astype(F32)
-                        + lax.dot_general(dk[rows, :], w3[n, :], NT, preferred_element_type=F32)
-                    ).astype(BF16)
+                tot[rows, :] = (up[rows, :].astype(F32) + acc[...]).astype(BF16)
 
             @pl.when(s >= 2)
             def _():
@@ -398,10 +398,6 @@
     @pl.when(s == 3)
     def _():
         forward(1)
-
-    @pl.when(s == 1)
-    def _():
-        product(dk)
 
     @pl.when(s >= 2)
     def _():
@@ -554,11 +550,13 @@
         kernel,
         name="window",
         out_shape=outs,
-        in_specs=[vmem, vmem, pl.BlockSpec(memory_space=pltpu.SMEM), vmem, hbm, hbm, hbm],
+        in_specs=[hbm, hbm, pl.BlockSpec(memory_space=pltpu.SMEM), hbm, hbm, hbm, hbm],
         out_specs=[vmem] * 5,
         scratch_shapes=[
             weight, weight, weight,
+            pltpu.VMEM((1000, C), BF16),
             pltpu.VMEM((2, 1, C), F32),
+            pltpu.VMEM((R, C), F32),
             act, act, act, act,
             pltpu.VMEM((rows, C), F32),
             act, act, act,
@@ -575,7 +573,7 @@
             sums, sums, sums,
             pltpu.VMEM((2, 2, 4, 40, Q), BF16),
             halves, halves, halves,
-            dma((3,)),
+            dma((4,)),
             pltpu.SemaphoreType.REGULAR,
             dma((2,)), dma((3,)),
             dma((2,)), dma((2,)),
@@ -590,10 +588,10 @@
             dma((2, 3)), dma((2, 3)),
         ],
         compiler_params=pltpu.CompilerParams(
-            collective_id=0, has_side_effects=True, vmem_limit_bytes=50_000_000
+            collective_id=0, has_side_effects=True, vmem_limit_bytes=54_000_000
         ),
     )(
-        latents.reshape(rows, C), cotangent.reshape(rows, C), timesteps, time_table.reshape(1000, C),
+        latents.reshape(rows, C), cotangent.reshape(rows, C), timesteps.reshape(2), time_table.reshape(1000, C),
         w_in.reshape(C, C), w_out.reshape(C, C), w_skip.reshape(C, C),
     )
     po, gi, g_in, g_out, g_skip = pl.pallas_call(

time: 111 us -> 107 us (0.964)
  local copies, waits for them, and re-layouts: 4.64 us -> 0.65 us
    unnamed x7 -> x2, local copies, waits for them, and re-layouts: 4.64 us -> 0.65 us
where the time goes in v4:
time: 107 us; the launch traced here: 106 us
  Pallas kernels  105 us (98%)
    pallas_call x1, Pallas kernels, body(): pl.pallas_call(kernel, name='window', out_shape=outs, in_specs=[hbm, hbm,...  104 us

profile of v4, /device:TPU:0, one launch (start us, length us, event | category | flops | bytes accessed | tf_op | source)
XLA Modules:
  0.0 106.4 jit_solution(7604489531135020050)
XLA Ops:
  0.6 0.0 copy-start
  0.6 0.6 copy-done
  1.3 103.8 %window.1 = (bf16[256,1280]{1,0:T(8,128)(2,1)S(1)}, bf16[256,1280]{1,0:T(8,128)(2,1)S(1)}, f32[40,1280]{1,0:T(8,128)S(1)}, f32[40,1280]{1,0:T(8,128)S(1)}, f32[40,1280]{1,0:T(8,128)S(1)}) custom-call(bf16[256,1280]{1,0:T(8,128)(2,1)} %bitcast.17, bf16[256,1280]{1,0:T(8,128)(2,1)} %bitcast.18, s32[2]{0:T(128)S(1)} %bitcast.12, bf16[1000,1280]{1,0:T(8,128)(2,1)} %bitcast.16, ...), custom_call_target="tpu_custom_call" | custom-call | tf_op jit(solution)/shard_map/window/pallas_call | solution.py:549
  105.1 1.3 %deliver.1 = (bf16[256,1280]{1,0:T(8,128)(2,1)}, bf16[256,1280]{1,0:T(8,128)(2,1)}, f32[40,1280]{1,0:T(8,128)}, f32[40,1280]{1,0:T(8,128)}, f32[40,1280]{1,0:T(8,128)}) custom-call(bf16[256,1280]{1,0:T(8,128)(2,1)S(1)} %get-tuple-element.15.refs_0_, bf16[256,1280]{1,0:T(8,128)(2,1)S(1)} %get-tuple-element.16.refs_1_, ...), custom_call_target="tpu_custom_call" | custom-call | tf_op jit(solution)/shard_map/deliver/pallas_call | solution.py:597
Async XLA Ops:
  0.6 0.7 copy-start

commit v5 on v4

--- a/solution.py
+++ b/solution.py
@@ -11,7 +11,6 @@
 C = 1280
 R = 128
 TILE = 256
-NT = (((1,), (1,)), ((), ()))
 BLOCKS = ((0, 0, 384, 0, 1), (1, 384, 256, 0, -1), (2, 640, 256, 1, 1), (3, 896, 384, 1, -1))
 Q = C // 4
 
@@ -19,7 +18,7 @@
 def kernel(
     lat, cot, steps, table, w_in, w_out, w_skip,
     po, gi, g_in, g_out, g_skip,
-    w1, w2, w3, rows_t, bias, acc, x, up, sk, dk, pre, gat, tot, dpre, lt, grads, r1, r2, r3, s1, q1, q2, q3, xs, xr,
+    w1, w2, w3, wt, rows_t, bias, acc, x, up, sk, dk, pre, gat, tot, dpre, lt, grads, r1, r2, r3, s1, q1, q2, q3, xs, xr,
     left, stage, right, part, p1, p2, p3, hs, hr, fs, fr,
     wsem, turn, x_s, x_r, sk_s, sk_r, up_s, up_r, dk_s, dk_r, rs_s, rs_r, xh_s, xh_r,
     ag_s, ag_r, fw_s, fw_r, aa_s, aa_r, js_s, js_r, fin_s, fin_r,
@@ -120,13 +119,10 @@
         return ring(1, 2, block, s1.at[(pos - by + 4) % 4, :, cols], q3.at[:, cols], axis, -by)
 
     def product(other):
-        @pl.loop(0, 4)
-        def _(zp):
-            mine = lt[pl.ds(pl.multiple_of(zp * 320, 320), 320), :]
-            for n in columns:
-                acc = jnp.dot(mine, other[:, n], preferred_element_type=F32).astype(BF16)
-                for yp in range(4):
-                    grads[zp, yp, :, n] = acc[yp * 80 : (yp + 1) * 80]
+        for n in columns:
+            whole = jnp.dot(lt[...], other[:, n], preferred_element_type=F32).astype(BF16)
+            for j in range(16):
+                grads[j // 4, j % 4, :, n] = whole[j * 80 : (j + 1) * 80]
 
         for block in BLOCKS:
             first(block, 0).start()
@@ -185,17 +181,10 @@
         return remote(part.at[job, o, (pos - by + 4) % 4], p3.at[job, o], *sems, axis, -by)
 
     def block_product(job):
-        @pl.loop(0, 4)
-        def _(zp):
-            acc = jnp.dot(
-                left[job, pl.ds(pl.multiple_of(zp * 320, 320), 320), :], right[job],
-                preferred_element_type=F32,
-            ).astype(BF16)
-            for yp in range(4):
-                if job == 0:
-                    part[0, zp, yp] = acc[yp * 80 : (yp + 1) * 80]
-                else:
-                    part[1, yp, zp] = acc[yp * 80 : (yp + 1) * 80]
+        whole = jnp.dot(left[job], right[job], preferred_element_type=F32).astype(BF16)
+        for j in range(16):
+            at = (j // 4, j % 4) if job == 0 else (j % 4, j // 4)
+            part[job, *at] = whole[j * 80 : (j + 1) * 80]
 
         for half in range(2):
             sums(job, half, 0).start()
@@ -220,6 +209,20 @@
         m = on3 * (i // 2) + (1 - on3) * (i % 2)
         rows = pl.ds(pl.multiple_of(m * R, R), R)
 
+        @pl.when((i == 0) & (s >= 2))
+        def _():
+            for n in (0, 2, 3):
+                loads[n].wait()
+
+        @pl.when(i == 2 * (1 - s // 2))
+        def _():
+            @pl.loop(0, C // TILE)
+            def _(j):
+                span = pl.ds(pl.multiple_of(j * TILE, TILE), TILE)
+                for k, w in enumerate((w1, w2, w3)):
+                    for n in columns:
+                        wt[k, n, span] = w[span, n].T
+
         @pl.when(kind == 0)
         def _():
             @pl.when((s == 0) & (m == 0))
@@ -230,7 +233,7 @@
             def _():
                 send_x(m).wait_recv()
 
-            @pl.when(i == 0)
+            @pl.when((i == 0) & (s < 2))
             def _():
                 loads[0].wait()
 
@@ -246,8 +249,11 @@
                 found = jnp.dot(hot.astype(F32).astype(BF16), rows_t[...], preferred_element_type=F32)
                 bias[0] = found[0:1]
                 bias[1] = found[1:2]
-                loads[2].wait()
-                loads[3].wait()
+
+                @pl.when(s < 2)
+                def _():
+                    loads[2].wait()
+                    loads[3].wait()
 
             @pl.when(s >= 2)
             def _():
@@ -310,9 +316,7 @@
             def _():
                 send_dk(m).wait_recv()
                 for n in columns:
-                    acc[:, n] = lax.dot_general(
-                        dk[rows, :], w3[n, :], NT, preferred_element_type=F32
-                    )
+                    acc[:, n] = jnp.dot(dk[rows, :], wt[2, :, n], preferred_element_type=F32)
 
                 @pl.when(m == 1)
                 def _():
@@ -332,7 +336,7 @@
 
             for n in columns:
                 dpre[rows, n] = (
-                    lax.dot_general(tot[rows, :], w2[n, :], NT, preferred_element_type=F32)
+                    jnp.dot(tot[rows, :], wt[1, :, n], preferred_element_type=F32)
                     * pre[rows, n]
                 ).astype(BF16)
 
@@ -344,15 +348,15 @@
             @pl.when(s == 2)
             def _():
                 for n in columns:
-                    dk[rows, n] = lax.dot_general(
-                        dpre[rows, :], w3[n, :], NT, preferred_element_type=F32
+                    dk[rows, n] = jnp.dot(
+                        dpre[rows, :], wt[2, :, n], preferred_element_type=F32
                     ).astype(BF16)
                 send_dk(m).start()
 
             for n in columns:
                 gi[rows, n] = (
                     tot[rows, n].astype(F32)
-                    + lax.dot_general(dpre[rows, :], w1[n, :], NT, preferred_element_type=F32)
+                    + jnp.dot(dpre[rows, :], wt[0, :, n], preferred_element_type=F32)
                 ).astype(BF16)
 
             @pl.when(s > 0)
@@ -362,8 +366,8 @@
             @pl.when(s == 3)
             def _():
                 for n in columns:
-                    dk[rows, n] = lax.dot_general(
-                        dpre[rows, :], w3[n, :], NT, preferred_element_type=F32
+                    dk[rows, n] = jnp.dot(
+                        dpre[rows, :], wt[2, :, n], preferred_element_type=F32
                     ).astype(BF16)
                 send_dk(m).start()
 
@@ -410,8 +414,6 @@
             for by in (1, 2, 3):
                 turned(job, m, by).wait_recv()
 
-    gathered(1)
-    block_product(1)
     for block in BLOCKS:
         _, col, width, colour, by = block
         cols = pl.ds(col, width)
@@ -420,15 +422,6 @@
             r1[:, :, cols].astype(F32) + piece(block, here[colour] + by + 4)[...].astype(F32)
         ).astype(BF16)
         first(block, 1).start()
-    gathered(0)
-    block_product(0)
-    for job in (1, 0):
-        for half in range(2):
-            o = pl.ds(2 * half, 2)
-            sums(job, half, 0).wait_recv()
-            pos = (here[1 - job] + 5 - 2 * half) % 4
-            p1[job, o] = (p1[job, o].astype(F32) + part[job, o, pos].astype(F32)).astype(BF16)
-            sums(job, half, 1).start()
     for block in BLOCKS:
         _, col, width, colour, by = block
         cols = pl.ds(col, width)
@@ -441,6 +434,17 @@
         ).astype(BF16)
         second(block, 0).start()
         second(block, 2).start()
+    gathered(1)
+    block_product(1)
+    gathered(0)
+    block_product(0)
+    for job in (1, 0):
+        for half in range(2):
+            o = pl.ds(2 * half, 2)
+            sums(job, half, 0).wait_recv()
+            pos = (here[1 - job] + 5 - 2 * half) % 4
+            p1[job, o] = (p1[job, o].astype(F32) + part[job, o, pos].astype(F32)).astype(BF16)
+            sums(job, half, 1).start()
     for job in (1, 0):
         for half in range(2):
             sums(job, half, 1).wait_recv()
@@ -554,6 +558,7 @@
         out_specs=[vmem] * 5,
         scratch_shapes=[
             weight, weight, weight,
+            pltpu.VMEM((3, C, C), BF16),
             pltpu.VMEM((1000, C), BF16),
             pltpu.VMEM((2, 1, C), F32),
             pltpu.VMEM((R, C), F32),

time: 107 us -> 108 us (level)
  Pallas kernels: 105 us -> 107 us
    pallas_call x1, Pallas kernels: 104 us -> 105 us  [body(): pl.pallas_call(kernel, name='window', out_shape=outs, in_specs=[hbm, hbm,...]
where the time goes in v5:
time: 108 us
  Pallas kernels  107 us (99%)
    pallas_call x1, Pallas kernels, body(): pl.pallas_call(kernel, name='window', out_shape=outs, in_specs=[hbm, hbm,...  105 us

profile of v5, /device:TPU:0, one launch (start us, length us, event | category | flops | bytes accessed | tf_op | source)
XLA Modules:
  0.0 108.0 jit_solution(4918602721787810255)
XLA Ops:
  0.6 0.0 copy-start
  0.6 0.6 copy-done
  1.3 105.3 %window.1 = (bf16[256,1280]{1,0:T(8,128)(2,1)S(1)}, bf16[256,1280]{1,0:T(8,128)(2,1)S(1)}, f32[40,1280]{1,0:T(8,128)S(1)}, f32[40,1280]{1,0:T(8,128)S(1)}, f32[40,1280]{1,0:T(8,128)S(1)}) custom-call(bf16[256,1280]{1,0:T(8,128)(2,1)} %bitcast.17, bf16[256,1280]{1,0:T(8,128)(2,1)} %bitcast.18, s32[2]{0:T(128)S(1)} %bitcast.12, bf16[1000,1280]{1,0:T(8,128)(2,1)} %bitcast.16, ...), custom_call_target="tpu_custom_call" | custom-call | tf_op jit(solution)/shard_map/window/pallas_call | solution.py:553
  106.6 1.3 %deliver.1 = (bf16[256,1280]{1,0:T(8,128)(2,1)}, bf16[256,1280]{1,0:T(8,128)(2,1)}, f32[40,1280]{1,0:T(8,128)}, f32[40,1280]{1,0:T(8,128)}, f32[40,1280]{1,0:T(8,128)}) custom-call(bf16[256,1280]{1,0:T(8,128)(2,1)S(1)} %get-tuple-element.15.refs_0_, bf16[256,1280]{1,0:T(8,128)(2,1)S(1)} %get-tuple-element.16.refs_1_, ...), custom_call_target="tpu_custom_call" | custom-call | tf_op jit(solution)/shard_map/deliver/pallas_call | solution.py:602
Async XLA Ops:
  0.6 0.7 copy-start

commit v6 on v5

--- a/solution.py
+++ b/solution.py
@@ -13,6 +13,7 @@
 TILE = 256
 BLOCKS = ((0, 0, 384, 0, 1), (1, 384, 256, 0, -1), (2, 640, 256, 1, 1), (3, 896, 384, 1, -1))
 Q = C // 4
+WIDE = 384
 
 
 def kernel(
@@ -163,7 +164,8 @@
         rows = pl.ds(pl.multiple_of(m * R, R), R)
         value = (dpre, tot)[job]
         for q in range(4):
-            stage[job, q, rows, :] = value[rows, q * Q : (q + 1) * Q]
+            stage[job, q, rows, :Q] = value[rows, q * Q : (q + 1) * Q]
+            stage[job, q, rows, Q:] = jnp.zeros((R, WIDE - Q), BF16)
         for by in (1, 3, 2):
             turned(job, m, by).start()
         right[job, slot(job, m), :] = stage[job, here[job], rows, :]
@@ -318,10 +320,6 @@
                 for n in columns:
                     acc[:, n] = jnp.dot(dk[rows, :], wt[2, :, n], preferred_element_type=F32)
 
-                @pl.when(m == 1)
-                def _():
-                    product(dk)
-
             @pl.when(s < 3)
             def _():
                 send_up(m).wait_recv()
@@ -395,13 +393,21 @@
                 for n in columns:
                     lt[n, rows] = sk[rows, n].T
 
-        @pl.when((i >= 1 + 2 * on3) & (i <= 2 + on3))
-        def _():
-            forward(i - 1 - 2 * on3)
+        @pl.when(i == 1 + 2 * on3)
+        def _():
+            forward(0)
+
+        @pl.when(((i == 1) & (s < 2)) | ((i == 2) & (s == 2)))
+        def _():
+            forward(1)
 
     @pl.when(s == 3)
     def _():
         forward(1)
+
+    @pl.when(s < 2)
+    def _():
+        product(dk)
 
     @pl.when(s >= 2)
     def _():
@@ -414,26 +420,6 @@
             for by in (1, 2, 3):
                 turned(job, m, by).wait_recv()
 
-    for block in BLOCKS:
-        _, col, width, colour, by = block
-        cols = pl.ds(col, width)
-        first(block, 0).wait_recv()
-        r1[:, :, cols] = (
-            r1[:, :, cols].astype(F32) + piece(block, here[colour] + by + 4)[...].astype(F32)
-        ).astype(BF16)
-        first(block, 1).start()
-    for block in BLOCKS:
-        _, col, width, colour, by = block
-        cols = pl.ds(col, width)
-        first(block, 1).wait_recv()
-        first(block, 2).wait_recv()
-        s1[:, :, cols] = (
-            piece(block, here[colour])[...].astype(F32)
-            + r2[:, :, cols].astype(F32)
-            + r3[:, :, cols].astype(F32)
-        ).astype(BF16)
-        second(block, 0).start()
-        second(block, 2).start()
     gathered(1)
     block_product(1)
     gathered(0)
@@ -445,6 +431,14 @@
             pos = (here[1 - job] + 5 - 2 * half) % 4
             p1[job, o] = (p1[job, o].astype(F32) + part[job, o, pos].astype(F32)).astype(BF16)
             sums(job, half, 1).start()
+    for block in BLOCKS:
+        _, col, width, colour, by = block
+        cols = pl.ds(col, width)
+        first(block, 0).wait_recv()
+        r1[:, :, cols] = (
+            r1[:, :, cols].astype(F32) + piece(block, here[colour] + by + 4)[...].astype(F32)
+        ).astype(BF16)
+        first(block, 1).start()
     for job in (1, 0):
         for half in range(2):
             sums(job, half, 1).wait_recv()
@@ -458,6 +452,18 @@
                 hs[job, 0, o] = total[:40].astype(BF16)
                 hs[job, 1, o] = total[40:].astype(BF16)
         pair(job).start()
+    for block in BLOCKS:
+        _, col, width, colour, by = block
+        cols = pl.ds(col, width)
+        first(block, 1).wait_recv()
+        first(block, 2).wait_recv()
+        s1[:, :, cols] = (
+            piece(block, here[colour])[...].astype(F32)
+            + r2[:, :, cols].astype(F32)
+            + r3[:, :, cols].astype(F32)
+        ).astype(BF16)
+        second(block, 0).start()
+        second(block, 2).start()
     for block in BLOCKS:
         _, col, width, colour, by = block
         cols = pl.ds(col, width)
@@ -489,7 +495,7 @@
         for by in (1, 2, 3):
             last(job, by).wait_recv()
         for q in range(4):
-            (g_in, g_out)[job][:, q * Q : (q + 1) * Q] = fr[job, q].astype(F32)
+            (g_in, g_out)[job][:, q * Q : (q + 1) * Q] = fr[job, q, :, :Q].astype(F32)
     pair(2).wait_recv()
     g_skip[...] = xs[xh].astype(F32) + xr[...].astype(F32)
     for block in BLOCKS:
@@ -544,8 +550,8 @@
     weight = pltpu.VMEM((C, C), BF16)
     quarter = pltpu.VMEM((4, 80, C), BF16)
     sixteenth = pltpu.VMEM((80, C), BF16)
-    sums = pltpu.VMEM((2, 4, 80, Q), BF16)
-    halves = pltpu.VMEM((2, 4, 40, Q), BF16)
+    sums = pltpu.VMEM((2, 4, 80, WIDE), BF16)
+    halves = pltpu.VMEM((2, 4, 40, WIDE), BF16)
     dma = pltpu.SemaphoreType.DMA
     out_act = jax.ShapeDtypeStruct((rows, C), BF16)
     out_grad = jax.ShapeDtypeStruct((40, C), F32)
@@ -572,11 +578,11 @@
             pltpu.VMEM((2, 40, C), BF16),
             pltpu.VMEM((40, C), BF16),
             pltpu.VMEM((2, C, 4 * rows), BF16),
-            pltpu.VMEM((2, 4, rows, Q), BF16),
-            pltpu.VMEM((2, 4 * rows, Q), BF16),
-            pltpu.VMEM((2, 4, 4, 80, Q), BF16),
+            pltpu.VMEM((2, 4, rows, WIDE), BF16),
+            pltpu.VMEM((2, 4 * rows, WIDE), BF16),
+            pltpu.VMEM((2, 4, 4, 80, WIDE), BF16),
             sums, sums, sums,
-            pltpu.VMEM((2, 2, 4, 40, Q), BF16),
+            pltpu.VMEM((2, 2, 4, 40, WIDE), BF16),
             halves, halves, halves,
             dma((4,)),
             pltpu.SemaphoreType.REGULAR,

time: 108 us -> 103 us (0.954)
  Pallas kernels: 107 us -> 101 us
    pallas_call x1, Pallas kernels: 105 us -> 100 us  [body(): pl.pallas_call(kernel, name='window', out_shape=outs, in_specs=[hbm, hbm,...]
where the time goes in v6:
time: 103 us
  Pallas kernels  101 us (98%)
    pallas_call x1, Pallas kernels, body(): pl.pallas_call(kernel, name='window', out_shape=outs, in_specs=[hbm, hbm,...  100 us

profile of v6, /device:TPU:0, one launch (start us, length us, event | category | flops | bytes accessed | tf_op | source)
XLA Modules:
  0.0 102.9 jit_solution(15251739606434098588)
XLA Ops:
  0.6 0.0 copy-start
  0.6 0.6 copy-done
  1.3 100.1 %window.1 = (bf16[256,1280]{1,0:T(8,128)(2,1)S(1)}, bf16[256,1280]{1,0:T(8,128)(2,1)S(1)}, f32[40,1280]{1,0:T(8,128)S(1)}, f32[40,1280]{1,0:T(8,128)S(1)}, f32[40,1280]{1,0:T(8,128)S(1)}) custom-call(bf16[256,1280]{1,0:T(8,128)(2,1)} %bitcast.17, bf16[256,1280]{1,0:T(8,128)(2,1)} %bitcast.18, s32[2]{0:T(128)S(1)} %bitcast.12, bf16[1000,1280]{1,0:T(8,128)(2,1)} %bitcast.16, ...), custom_call_target="tpu_custom_call" | custom-call | tf_op jit(solution)/shard_map/window/pallas_call | solution.py:559
  101.4 1.3 %deliver.1 = (bf16[256,1280]{1,0:T(8,128)(2,1)}, bf16[256,1280]{1,0:T(8,128)(2,1)}, f32[40,1280]{1,0:T(8,128)}, f32[40,1280]{1,0:T(8,128)}, f32[40,1280]{1,0:T(8,128)}) custom-call(bf16[256,1280]{1,0:T(8,128)(2,1)S(1)} %get-tuple-element.15.refs_0_, bf16[256,1280]{1,0:T(8,128)(2,1)S(1)} %get-tuple-element.16.refs_1_, ...), custom_call_target="tpu_custom_call" | custom-call | tf_op jit(solution)/shard_map/deliver/pallas_call | solution.py:608
Async XLA Ops:
  0.6 0.7 copy-start

commit v7 on v6

--- a/solution.py
+++ b/solution.py
@@ -11,7 +11,7 @@
 C = 1280
 R = 128
 TILE = 256
-BLOCKS = ((0, 0, 384, 0, 1), (1, 384, 256, 0, -1), (2, 640, 256, 1, 1), (3, 896, 384, 1, -1))
+AXES = (0, 1, 0)
 Q = C // 4
 WIDE = 384
 
@@ -19,9 +19,9 @@
 def kernel(
     lat, cot, steps, table, w_in, w_out, w_skip,
     po, gi, g_in, g_out, g_skip,
-    w1, w2, w3, wt, rows_t, bias, acc, x, up, sk, dk, pre, gat, tot, dpre, lt, grads, r1, r2, r3, s1, q1, q2, q3, xs, xr,
+    w1, w2, w3, wt, rows_t, bias, acc, x, up, sk, dk, pre, gat, tot, dpre,
     left, stage, right, part, p1, p2, p3, hs, hr, fs, fr,
-    wsem, turn, x_s, x_r, sk_s, sk_r, up_s, up_r, dk_s, dk_r, rs_s, rs_r, xh_s, xh_r,
+    wsem, turn, x_s, x_r, sk_s, sk_r, up_s, up_r, dk_s, dk_r, xh_s, xh_r,
     ag_s, ag_r, fw_s, fw_r, aa_s, aa_r, js_s, js_r, fin_s, fin_r,
 ):
     s = lax.axis_index("segment")
@@ -84,51 +84,6 @@
 
     here = (z, y)
 
-    def ring(step, msg, block, src, dst, axis, by):
-        n = block[0]
-        return pltpu.make_async_remote_copy(
-            src_ref=src, dst_ref=dst, send_sem=rs_s.at[step, msg, n], recv_sem=rs_r.at[step, msg, n],
-            device_id={"dp": along(axis, by)}, device_id_type=MESH,
-        )
-
-    def piece(block, pos):
-        _, col, width, colour, _ = block
-        cols = pl.ds(col, width)
-        if colour == 0:
-            return grads.at[pos % 4, :, :, cols]
-        return grads.at[:, pos % 4, :, cols]
-
-    def first(block, msg):
-        _, col, width, colour, by = block
-        cols = pl.ds(col, width)
-        pos = here[colour]
-        if msg == 0:
-            return ring(0, 0, block, piece(block, pos + 2), r1.at[:, :, cols], colour, by)
-        if msg == 1:
-            return ring(0, 1, block, r1.at[:, :, cols], r2.at[:, :, cols], colour, by)
-        return ring(0, 2, block, piece(block, pos - by + 4), r3.at[:, :, cols], colour, -by)
-
-    def second(block, msg):
-        _, col, width, colour, by = block
-        cols = pl.ds(col, width)
-        axis = 1 - colour
-        pos = here[axis]
-        if msg == 0:
-            return ring(1, 0, block, s1.at[(pos + 2) % 4, :, cols], q1.at[:, cols], axis, by)
-        if msg == 1:
-            return ring(1, 1, block, q1.at[:, cols], q2.at[:, cols], axis, by)
-        return ring(1, 2, block, s1.at[(pos - by + 4) % 4, :, cols], q3.at[:, cols], axis, -by)
-
-    def product(other):
-        for n in columns:
-            whole = jnp.dot(lt[...], other[:, n], preferred_element_type=F32).astype(BF16)
-            for j in range(16):
-                grads[j // 4, j % 4, :, n] = whole[j * 80 : (j + 1) * 80]
-
-        for block in BLOCKS:
-            first(block, 0).start()
-            first(block, 2).start()
-
     def remote(src, dst, send, recv, axis, by):
         return pltpu.make_async_remote_copy(
             src_ref=src, dst_ref=dst, send_sem=send, recv_sem=recv,
@@ -136,19 +91,19 @@
         )
 
     def slot(job, m, by=0):
-        return pl.ds(pl.multiple_of(((here[job] + by + 4) % 4 * 2 + m) * R, R), R)
+        return pl.ds(pl.multiple_of(((here[AXES[job]] + by + 4) % 4 * 2 + m) * R, R), R)
 
     def spread(job, m, d):
         ref = left.at[job, :, slot(job, m)]
-        return remote(ref, ref, ag_s.at[job, m, d], ag_r.at[job, m, d], job, 1 - 2 * d)
+        return remote(ref, ref, ag_s.at[job, m, d], ag_r.at[job, m, d], AXES[job], 1 - 2 * d)
 
     def relay(job, m, d):
         by = 1 - 2 * d
         ref = left.at[job, pl.ds(d * 640, 640), slot(job, m, -by)]
-        return remote(ref, ref, fw_s.at[job, m, d], fw_r.at[job, m, d], job, by)
+        return remote(ref, ref, fw_s.at[job, m, d], fw_r.at[job, m, d], AXES[job], by)
 
     def forward(m):
-        for job in range(2):
+        for job in range(3):
             for d in range(2):
                 spread(job, m, d).wait_recv()
                 relay(job, m, d).start()
@@ -156,23 +111,23 @@
     def turned(job, m, by):
         rows = pl.ds(pl.multiple_of(m * R, R), R)
         return remote(
-            stage.at[job, (here[job] + by) % 4, rows], right.at[job, slot(job, m)],
-            aa_s.at[job, m, by - 1], aa_r.at[job, m, by - 1], job, by,
+            stage.at[job, (here[AXES[job]] + by) % 4, rows], right.at[job, slot(job, m)],
+            aa_s.at[job, m, by - 1], aa_r.at[job, m, by - 1], AXES[job], by,
         )
 
     def swap(job, m):
         rows = pl.ds(pl.multiple_of(m * R, R), R)
-        value = (dpre, tot)[job]
+        value = (dpre, tot, dk)[job]
         for q in range(4):
             stage[job, q, rows, :Q] = value[rows, q * Q : (q + 1) * Q]
             stage[job, q, rows, Q:] = jnp.zeros((R, WIDE - Q), BF16)
         for by in (1, 3, 2):
             turned(job, m, by).start()
-        right[job, slot(job, m), :] = stage[job, here[job], rows, :]
+        right[job, slot(job, m), :] = stage[job, here[AXES[job]], rows, :]
 
     def sums(job, half, msg):
         by = 1 - 2 * half
-        axis = 1 - job
+        axis = 1 - AXES[job]
         pos = here[axis]
         o = pl.ds(2 * half, 2)
         sems = (js_s.at[job, half, msg], js_r.at[job, half, msg])
@@ -183,9 +138,10 @@
         return remote(part.at[job, o, (pos - by + 4) % 4], p3.at[job, o], *sems, axis, -by)
 
     def block_product(job):
-        whole = jnp.dot(left[job], right[job], preferred_element_type=F32).astype(BF16)
+        source = 2 - 2 * (s // 2) if job == 2 else job
+        whole = jnp.dot(left[job], right[source], preferred_element_type=F32).astype(BF16)
         for j in range(16):
-            at = (j // 4, j % 4) if job == 0 else (j % 4, j // 4)
+            at = (j // 4, j % 4) if AXES[job] == 0 else (j % 4, j // 4)
             part[job, *at] = whole[j * 80 : (j + 1) * 80]
 
         for half in range(2):
@@ -193,17 +149,24 @@
             sums(job, half, 2).start()
 
     def pair(k):
-        src, dst = ((hs.at[0, 1 - xh], hr.at[0]), (hs.at[1, 1 - xh], hr.at[1]), (xs.at[1 - xh], xr))[k]
         return pltpu.make_async_remote_copy(
-            src_ref=src, dst_ref=dst, send_sem=xh_s.at[k], recv_sem=xh_r.at[k],
+            src_ref=hs.at[k, 1 - xh], dst_ref=hr.at[k], send_sem=xh_s.at[k], recv_sem=xh_r.at[k],
             device_id={"dp": partner}, device_id_type=MESH,
         )
 
     def last(job, by):
         return remote(
-            fs.at[job, (here[job] + by) % 4], fr.at[job, here[job]],
-            fin_s.at[job, by - 1], fin_r.at[job, by - 1], job, by,
+            fs.at[job, (here[AXES[job]] + by) % 4], fr.at[job, here[AXES[job]]],
+            fin_s.at[job, by - 1], fin_r.at[job, by - 1], AXES[job], by,
         )
+
+    def turn_weights():
+        @pl.loop(0, C // TILE)
+        def _(j):
+            span = pl.ds(pl.multiple_of(j * TILE, TILE), TILE)
+            for k, w in enumerate((w1, w2, w3)):
+                for n in columns:
+                    wt[k, n, span] = w[span, n].T
 
     @pl.loop(0, 4)
     def _(i):
@@ -215,15 +178,7 @@
         def _():
             for n in (0, 2, 3):
                 loads[n].wait()
-
-        @pl.when(i == 2 * (1 - s // 2))
-        def _():
-            @pl.loop(0, C // TILE)
-            def _(j):
-                span = pl.ds(pl.multiple_of(j * TILE, TILE), TILE)
-                for k, w in enumerate((w1, w2, w3)):
-                    for n in columns:
-                        wt[k, n, span] = w[span, n].T
+            turn_weights()
 
         @pl.when(kind == 0)
         def _():
@@ -317,6 +272,7 @@
             @pl.when(s < 2)
             def _():
                 send_dk(m).wait_recv()
+                swap(2, m)
                 for n in columns:
                     acc[:, n] = jnp.dot(dk[rows, :], wt[2, :, n], preferred_element_type=F32)
 
@@ -379,141 +335,118 @@
             for n in columns:
                 left[0, n, slot(0, m)] = x[rows, n].T
                 left[1, n, slot(1, m)] = gat[rows, n].T
-            for job in range(2):
+
+            @pl.when(s < 2)
+            def _():
+                for n in columns:
+                    left[2, n, slot(2, m)] = po[rows, n].T
+
+            @pl.when(s >= 2)
+            def _():
+                for n in columns:
+                    left[2, n, slot(2, m)] = sk[rows, n].T
+
+            for job in range(3):
                 for d in range(2):
                     spread(job, m, d).start()
 
-            @pl.when(s < 2)
-            def _():
-                for n in columns:
-                    lt[n, rows] = po[rows, n].T
-
-            @pl.when(s >= 2)
-            def _():
-                for n in columns:
-                    lt[n, rows] = sk[rows, n].T
-
-        @pl.when(i == 1 + 2 * on3)
+        @pl.when((i == 1) & (s < 2))
         def _():
             forward(0)
-
-        @pl.when(((i == 1) & (s < 2)) | ((i == 2) & (s == 2)))
-        def _():
+            turn_weights()
             forward(1)
 
-    @pl.when(s == 3)
-    def _():
+    @pl.when(s >= 2)
+    def _():
+        forward(0)
         forward(1)
-
-    @pl.when(s < 2)
-    def _():
-        product(dk)
-
-    @pl.when(s >= 2)
-    def _():
-        product(dpre)
 
     def gathered(job):
         for m in range(2):
             for d in range(2):
                 relay(job, m, d).wait_recv()
+
+    def arrived(job):
+        for m in range(2):
             for by in (1, 2, 3):
                 turned(job, m, by).wait_recv()
 
-    gathered(1)
-    block_product(1)
-    gathered(0)
-    block_product(0)
-    for job in (1, 0):
+    def passed(job):
         for half in range(2):
             o = pl.ds(2 * half, 2)
             sums(job, half, 0).wait_recv()
-            pos = (here[1 - job] + 5 - 2 * half) % 4
+            pos = (here[1 - AXES[job]] + 5 - 2 * half) % 4
             p1[job, o] = (p1[job, o].astype(F32) + part[job, o, pos].astype(F32)).astype(BF16)
             sums(job, half, 1).start()
-    for block in BLOCKS:
-        _, col, width, colour, by = block
-        cols = pl.ds(col, width)
-        first(block, 0).wait_recv()
-        r1[:, :, cols] = (
-            r1[:, :, cols].astype(F32) + piece(block, here[colour] + by + 4)[...].astype(F32)
-        ).astype(BF16)
-        first(block, 1).start()
-    for job in (1, 0):
+
+    gathered(2)
+
+    @pl.when(s < 2)
+    def _():
+        arrived(2)
+
+    @pl.when(s >= 2)
+    def _():
+        arrived(0)
+
+    block_product(2)
+    gathered(1)
+    arrived(1)
+    block_product(1)
+    passed(2)
+    gathered(0)
+
+    @pl.when(s < 2)
+    def _():
+        arrived(0)
+
+    block_product(0)
+    passed(1)
+    passed(0)
+    for job in (2, 1, 0):
         for half in range(2):
             sums(job, half, 1).wait_recv()
             sums(job, half, 2).wait_recv()
             for o in (2 * half, 2 * half + 1):
                 total = (
-                    part[job, o, here[1 - job]].astype(F32)
+                    part[job, o, here[1 - AXES[job]]].astype(F32)
                     + p2[job, o].astype(F32)
                     + p3[job, o].astype(F32)
                 )
                 hs[job, 0, o] = total[:40].astype(BF16)
                 hs[job, 1, o] = total[40:].astype(BF16)
         pair(job).start()
-    for block in BLOCKS:
-        _, col, width, colour, by = block
-        cols = pl.ds(col, width)
-        first(block, 1).wait_recv()
-        first(block, 2).wait_recv()
-        s1[:, :, cols] = (
-            piece(block, here[colour])[...].astype(F32)
-            + r2[:, :, cols].astype(F32)
-            + r3[:, :, cols].astype(F32)
-        ).astype(BF16)
-        second(block, 0).start()
-        second(block, 2).start()
-    for block in BLOCKS:
-        _, col, width, colour, by = block
-        cols = pl.ds(col, width)
-        second(block, 0).wait_recv()
-        pos = (here[1 - colour] + by + 4) % 4
-        q1[:, cols] = (q1[:, cols].astype(F32) + s1[pos, :, cols].astype(F32)).astype(BF16)
-        second(block, 1).start()
-    for job in (1, 0):
+    for job in (2, 1, 0):
         pair(job).wait_recv()
         for o in range(4):
             fs[job, o] = (hs[job, xh, o].astype(F32) + hr[job, o].astype(F32)).astype(BF16)
         for by in (1, 3, 2):
             last(job, by).start()
-        fr[job, here[job]] = fs[job, here[job]]
-    for block in BLOCKS:
-        _, col, width, colour, by = block
-        cols = pl.ds(col, width)
-        second(block, 1).wait_recv()
-        second(block, 2).wait_recv()
-        total = (
-            s1[here[1 - colour], :, cols].astype(F32)
-            + q2[:, cols].astype(F32)
-            + q3[:, cols].astype(F32)
-        )
-        xs[0, :, cols] = total[:40].astype(BF16)
-        xs[1, :, cols] = total[40:].astype(BF16)
-    pair(2).start()
-    for job in (1, 0):
+        fr[job, here[AXES[job]]] = fs[job, here[AXES[job]]]
+    for job in (2, 1, 0):
         for by in (1, 2, 3):
             last(job, by).wait_recv()
         for q in range(4):
-            (g_in, g_out)[job][:, q * Q : (q + 1) * Q] = fr[job, q, :, :Q].astype(F32)
-    pair(2).wait_recv()
-    g_skip[...] = xs[xh].astype(F32) + xr[...].astype(F32)
-    for block in BLOCKS:
-        for msg in range(3):
-            first(block, msg).wait_send()
-            second(block, msg).wait_send()
-    for k in range(3):
-        pair(k).wait_send()
-    for job in range(2):
+            (g_in, g_out, g_skip)[job][:, q * Q : (q + 1) * Q] = fr[job, q, :, :Q].astype(F32)
+    for job in range(3):
+        pair(job).wait_send()
         for n in range(3):
             last(job, n + 1).wait_send()
-            for m in range(2):
-                turned(job, m, n + 1).wait_send()
+        for m in range(2):
+            for n in range(3):
                 sums(job, m, n).wait_send()
-        for m in range(2):
+                if job < 2:
+                    turned(job, m, n + 1).wait_send()
             for d in range(2):
                 spread(job, m, d).wait_send()
                 relay(job, m, d).wait_send()
+
+    @pl.when(s < 2)
+    def _():
+        for m in range(2):
+            for n in range(3):
+                turned(2, m, n + 1).wait_send()
+
     for m in range(2):
 
         @pl.when((s == 0) | (s == 2))
@@ -548,10 +481,8 @@
     hbm = pl.BlockSpec(memory_space=pltpu.HBM)
     act = pltpu.VMEM((rows, C), BF16)
     weight = pltpu.VMEM((C, C), BF16)
-    quarter = pltpu.VMEM((4, 80, C), BF16)
-    sixteenth = pltpu.VMEM((80, C), BF16)
-    sums = pltpu.VMEM((2, 4, 80, WIDE), BF16)
-    halves = pltpu.VMEM((2, 4, 40, WIDE), BF16)
+    sums = pltpu.VMEM((3, 4, 80, WIDE), BF16)
+    halves = pltpu.VMEM((3, 4, 40, WIDE), BF16)
     dma = pltpu.SemaphoreType.DMA
     out_act = jax.ShapeDtypeStruct((rows, C), BF16)
     out_grad = jax.ShapeDtypeStruct((40, C), F32)
@@ -571,18 +502,12 @@
             act, act, act, act,
             pltpu.VMEM((rows, C), F32),
             act, act, act,
-            pltpu.VMEM((C, rows), BF16),
-            pltpu.VMEM((4, 4, 80, C), BF16),
-            quarter, quarter, quarter, quarter,
-            sixteenth, sixteenth, sixteenth,
-            pltpu.VMEM((2, 40, C), BF16),
-            pltpu.VMEM((40, C), BF16),
-            pltpu.VMEM((2, C, 4 * rows), BF16),
-            pltpu.VMEM((2, 4, rows, WIDE), BF16),
-            pltpu.VMEM((2, 4 * rows, WIDE), BF16),
-            pltpu.VMEM((2, 4, 4, 80, WIDE), BF16),
+            pltpu.VMEM((3, C, 4 * rows), BF16),
+            pltpu.VMEM((3, 4, rows, WIDE), BF16),
+            pltpu.VMEM((3, 4 * rows, WIDE), BF16),
+            pltpu.VMEM((3, 4, 4, 80, WIDE), BF16),
             sums, sums, sums,
-            pltpu.VMEM((2, 2, 4, 40, WIDE), BF16),
+            pltpu.VMEM((3, 2, 4, 40, WIDE), BF16),
             halves, halves, halves,
             dma((4,)),
             pltpu.SemaphoreType.REGULAR,
@@ -590,13 +515,12 @@
             dma((2,)), dma((2,)),
             dma((2,)), dma((3,)),
             dma((2,)), dma((2,)),
-            dma((2, 3, 4)), dma((2, 3, 4)),
             dma((3,)), dma((3,)),
-            dma((2, 2, 2)), dma((2, 2, 2)),
-            dma((2, 2, 2)), dma((2, 2, 2)),
-            dma((2, 2, 3)), dma((2, 2, 3)),
-            dma((2, 2, 3)), dma((2, 2, 3)),
-            dma((2, 3)), dma((2, 3)),
+            dma((3, 2, 2)), dma((3, 2, 2)),
+            dma((3, 2, 2)), dma((3, 2, 2)),
+            dma((3, 2, 3)), dma((3, 2, 3)),
+            dma((3, 2, 3)), dma((3, 2, 3)),
+            dma((3, 3)), dma((3, 3)),
         ],
         compiler_params=pltpu.CompilerParams(
             collective_id=0, has_side_effects=True, vmem_limit_bytes=54_000_000

time: 103 us -> 111 us (1.078)
  the two profiles are of different devices: /device:TPU:0 before, /device:TPU:3 now
where the time goes in v7:
time: 111 us
  Pallas kernels  109 us (98%)
    pallas_call x1, Pallas kernels, body(): pl.pallas_call(kernel, name='window', out_shape=outs, in_specs=[hbm, hbm,...  108 us

profile of v7, /device:TPU:3, one launch (start us, length us, event | category | flops | bytes accessed | tf_op | source)
XLA Modules:
  0.0 110.9 jit_solution(3183530266281842250)
XLA Ops:
  0.6 0.0 copy-start
  0.6 0.6 copy-done
  1.3 108.1 %window.1 = (bf16[256,1280]{1,0:T(8,128)(2,1)S(1)}, bf16[256,1280]{1,0:T(8,128)(2,1)S(1)}, f32[40,1280]{1,0:T(8,128)S(1)}, f32[40,1280]{1,0:T(8,128)S(1)}, f32[40,1280]{1,0:T(8,128)S(1)}) custom-call(bf16[256,1280]{1,0:T(8,128)(2,1)} %bitcast.17, bf16[256,1280]{1,0:T(8,128)(2,1)} %bitcast.18, s32[2]{0:T(128)S(1)} %bitcast.12, bf16[1000,1280]{1,0:T(8,128)(2,1)} %bitcast.16, ...), custom_call_target="tpu_custom_call" | custom-call | tf_op jit(solution)/shard_map/window/pallas_call | solution.py:490
  109.4 1.3 %deliver.1 = (bf16[256,1280]{1,0:T(8,128)(2,1)}, bf16[256,1280]{1,0:T(8,128)(2,1)}, f32[40,1280]{1,0:T(8,128)}, f32[40,1280]{1,0:T(8,128)}, f32[40,1280]{1,0:T(8,128)}) custom-call(bf16[256,1280]{1,0:T(8,128)(2,1)S(1)} %get-tuple-element.15.refs_0_, bf16[256,1280]{1,0:T(8,128)(2,1)S(1)} %get-tuple-element.16.refs_1_, ...), custom_call_target="tpu_custom_call" | custom-call | tf_op jit(solution)/shard_map/deliver/pallas_call | solution.py:532
Async XLA Ops:
  0.6 0.7 copy-start

commit v8 on v6

--- a/solution.py
+++ b/solution.py
@@ -186,7 +186,8 @@
         whole = jnp.dot(left[job], right[job], preferred_element_type=F32).astype(BF16)
         for j in range(16):
             at = (j // 4, j % 4) if job == 0 else (j % 4, j // 4)
-            part[job, *at] = whole[j * 80 : (j + 1) * 80]
+            part[job, *at, :, :Q] = whole[j * 80 : j * 80 + 40, :Q]
+            part[job, *at, :, Q:] = whole[j * 80 + 40 : (j + 1) * 80, :Q]
 
         for half in range(2):
             sums(job, half, 0).start()
@@ -320,6 +321,10 @@
                 for n in columns:
                     acc[:, n] = jnp.dot(dk[rows, :], wt[2, :, n], preferred_element_type=F32)
 
+                @pl.when((m == 1) & (s < 2))
+                def _():
+                    product(dk)
+
             @pl.when(s < 3)
             def _():
                 send_up(m).wait_recv()
@@ -405,10 +410,6 @@
     def _():
         forward(1)
 
-    @pl.when(s < 2)
-    def _():
-        product(dk)
-
     @pl.when(s >= 2)
     def _():
         product(dpre)
@@ -420,6 +421,14 @@
             for by in (1, 2, 3):
                 turned(job, m, by).wait_recv()
 
+    for block in BLOCKS:
+        _, col, width, colour, by = block
+        cols = pl.ds(col, width)
+        first(block, 0).wait_recv()
+        r1[:, :, cols] = (
+            r1[:, :, cols].astype(F32) + piece(block, here[colour] + by + 4)[...].astype(F32)
+        ).astype(BF16)
+        first(block, 1).start()
     gathered(1)
     block_product(1)
     gathered(0)
@@ -431,14 +440,6 @@
             pos = (here[1 - job] + 5 - 2 * half) % 4
             p1[job, o] = (p1[job, o].astype(F32) + part[job, o, pos].astype(F32)).astype(BF16)
             sums(job, half, 1).start()
-    for block in BLOCKS:
-        _, col, width, colour, by = block
-        cols = pl.ds(col, width)
-        first(block, 0).wait_recv()
-        r1[:, :, cols] = (
-            r1[:, :, cols].astype(F32) + piece(block, here[colour] + by + 4)[...].astype(F32)
-        ).astype(BF16)
-        first(block, 1).start()
     for job in (1, 0):
         for half in range(2):
             sums(job, half, 1).wait_recv()
@@ -449,8 +450,9 @@
                     + p2[job, o].astype(F32)
                     + p3[job, o].astype(F32)
                 )
-                hs[job, 0, o] = total[:40].astype(BF16)
-                hs[job, 1, o] = total[40:].astype(BF16)
+                lanes = pl.ds(o % 2 * Q, Q)
+                hs[job, 0, half, :, lanes] = total[:, :Q].astype(BF16)
+                hs[job, 1, half, :, lanes] = total[:, Q:].astype(BF16)
         pair(job).start()
     for block in BLOCKS:
         _, col, width, colour, by = block
@@ -474,7 +476,10 @@
     for job in (1, 0):
         pair(job).wait_recv()
         for o in range(4):
-            fs[job, o] = (hs[job, xh, o].astype(F32) + hr[job, o].astype(F32)).astype(BF16)
+            lanes = pl.ds(o % 2 * Q, Q)
+            mine = hs[job, xh, o // 2, :, lanes].astype(F32)
+            fs[job, o, :, :Q] = (mine + hr[job, o // 2, :, lanes].astype(F32)).astype(BF16)
+            fs[job, o, :, Q:] = jnp.zeros((40, WIDE - Q), BF16)
         for by in (1, 3, 2):
             last(job, by).start()
         fr[job, here[job]] = fs[job, here[job]]
@@ -550,7 +555,7 @@
     weight = pltpu.VMEM((C, C), BF16)
     quarter = pltpu.VMEM((4, 80, C), BF16)
     sixteenth = pltpu.VMEM((80, C), BF16)
-    sums = pltpu.VMEM((2, 4, 80, WIDE), BF16)
+    sums = pltpu.VMEM((2, 4, 40, 2 * Q), BF16)
     halves = pltpu.VMEM((2, 4, 40, WIDE), BF16)
     dma = pltpu.SemaphoreType.DMA
     out_act = jax.ShapeDtypeStruct((rows, C), BF16)
@@ -580,10 +585,11 @@
             pltpu.VMEM((2, C, 4 * rows), BF16),
             pltpu.VMEM((2, 4, rows, WIDE), BF16),
             pltpu.VMEM((2, 4 * rows, WIDE), BF16),
-            pltpu.VMEM((2, 4, 4, 80, WIDE), BF16),
+            pltpu.VMEM((2, 4, 4, 40, 2 * Q), BF16),
             sums, sums, sums,
-            pltpu.VMEM((2, 2, 4, 40, WIDE), BF16),
-            halves, halves, halves,
+            pltpu.VMEM((2, 2, 2, 40, 2 * Q), BF16),
+            pltpu.VMEM((2, 2, 40, 2 * Q), BF16),
+            halves, halves,
             dma((4,)),
             pltpu.SemaphoreType.REGULAR,
             dma((2,)), dma((3,)),

time: 103 us -> 100 us (0.971)
  Pallas kernels: 101 us -> 98.3 us
    pallas_call x1, Pallas kernels: 100 us -> 97 us  [body(): pl.pallas_call(kernel, name='window', out_shape=outs, in_specs=[hbm, hbm,...]
where the time goes in v8:
time: 100 us; the launch traced here: 99.8 us
  Pallas kernels  98.3 us (98%)
    pallas_call x1, Pallas kernels, body(): pl.pallas_call(kernel, name='window', out_shape=outs, in_specs=[hbm, hbm,...  97 us

profile of v8, /device:TPU:0, one launch (start us, length us, event | category | flops | bytes accessed | tf_op | source)
XLA Modules:
  0.0 99.8 jit_solution(3237396693948895450)
XLA Ops:
  0.6 0.0 copy-start
  0.6 0.6 copy-done
  1.3 97.0 %window.1 = (bf16[256,1280]{1,0:T(8,128)(2,1)S(1)}, bf16[256,1280]{1,0:T(8,128)(2,1)S(1)}, f32[40,1280]{1,0:T(8,128)S(1)}, f32[40,1280]{1,0:T(8,128)S(1)}, f32[40,1280]{1,0:T(8,128)S(1)}) custom-call(bf16[256,1280]{1,0:T(8,128)(2,1)} %bitcast.17, bf16[256,1280]{1,0:T(8,128)(2,1)} %bitcast.18, s32[2]{0:T(128)S(1)} %bitcast.12, bf16[1000,1280]{1,0:T(8,128)(2,1)} %bitcast.16, ...), custom_call_target="tpu_custom_call" | custom-call | tf_op jit(solution)/shard_map/window/pallas_call | solution.py:564
  98.3 1.3 %deliver.1 = (bf16[256,1280]{1,0:T(8,128)(2,1)}, bf16[256,1280]{1,0:T(8,128)(2,1)}, f32[40,1280]{1,0:T(8,128)}, f32[40,1280]{1,0:T(8,128)}, f32[40,1280]{1,0:T(8,128)}) custom-call(bf16[256,1280]{1,0:T(8,128)(2,1)S(1)} %get-tuple-element.15.refs_0_, bf16[256,1280]{1,0:T(8,128)(2,1)S(1)} %get-tuple-element.16.refs_1_, ...), custom_call_target="tpu_custom_call" | custom-call | tf_op jit(solution)/shard_map/deliver/pallas_call | solution.py:614
Async XLA Ops:
  0.6 0.7 copy-start

commit v9 on v8

--- a/solution.py
+++ b/solution.py
@@ -421,14 +421,20 @@
             for by in (1, 2, 3):
                 turned(job, m, by).wait_recv()
 
-    for block in BLOCKS:
-        _, col, width, colour, by = block
-        cols = pl.ds(col, width)
-        first(block, 0).wait_recv()
-        r1[:, :, cols] = (
-            r1[:, :, cols].astype(F32) + piece(block, here[colour] + by + 4)[...].astype(F32)
-        ).astype(BF16)
-        first(block, 1).start()
+    def relayed():
+        for block in BLOCKS:
+            _, col, width, colour, by = block
+            cols = pl.ds(col, width)
+            first(block, 0).wait_recv()
+            r1[:, :, cols] = (
+                r1[:, :, cols].astype(F32) + piece(block, here[colour] + by + 4)[...].astype(F32)
+            ).astype(BF16)
+            first(block, 1).start()
+
+    @pl.when(s < 2)
+    def _():
+        relayed()
+
     gathered(1)
     block_product(1)
     gathered(0)
@@ -440,6 +446,10 @@
             pos = (here[1 - job] + 5 - 2 * half) % 4
             p1[job, o] = (p1[job, o].astype(F32) + part[job, o, pos].astype(F32)).astype(BF16)
             sums(job, half, 1).start()
+    @pl.when(s >= 2)
+    def _():
+        relayed()
+
     for job in (1, 0):
         for half in range(2):
             sums(job, half, 1).wait_recv()

time: 100 us -> 99.9 us (level)
  no operation moved by 1% of the time
where the time goes in v9:
time: 99.9 us; the launch traced here: 99.6 us
  Pallas kernels  98.3 us (98%)
    pallas_call x1, Pallas kernels, body(): pl.pallas_call(kernel, name='window', out_shape=outs, in_specs=[hbm, hbm,...  97 us

profile of v9, /device:TPU:0, one launch (start us, length us, event | category | flops | bytes accessed | tf_op | source)
XLA Modules:
  0.0 99.6 jit_solution(5097883973673063401)
XLA Ops:
  0.6 0.0 copy-start
  0.6 0.6 copy-done
  1.3 97.0 %window.1 = (bf16[256,1280]{1,0:T(8,128)(2,1)S(1)}, bf16[256,1280]{1,0:T(8,128)(2,1)S(1)}, f32[40,1280]{1,0:T(8,128)S(1)}, f32[40,1280]{1,0:T(8,128)S(1)}, f32[40,1280]{1,0:T(8,128)S(1)}) custom-call(bf16[256,1280]{1,0:T(8,128)(2,1)} %bitcast.17, bf16[256,1280]{1,0:T(8,128)(2,1)} %bitcast.18, s32[2]{0:T(128)S(1)} %bitcast.12, bf16[1000,1280]{1,0:T(8,128)(2,1)} %bitcast.16, ...), custom_call_target="tpu_custom_call" | custom-call | tf_op jit(solution)/shard_map/window/pallas_call | solution.py:574
  98.3 1.3 %deliver.1 = (bf16[256,1280]{1,0:T(8,128)(2,1)}, bf16[256,1280]{1,0:T(8,128)(2,1)}, f32[40,1280]{1,0:T(8,128)}, f32[40,1280]{1,0:T(8,128)}, f32[40,1280]{1,0:T(8,128)}) custom-call(bf16[256,1280]{1,0:T(8,128)(2,1)S(1)} %get-tuple-element.15.refs_0_, bf16[256,1280]{1,0:T(8,128)(2,1)S(1)} %get-tuple-element.16.refs_1_, ...), custom_call_target="tpu_custom_call" | custom-call | tf_op jit(solution)/shard_map/deliver/pallas_call | solution.py:624
Async XLA Ops:
  0.6 0.7 copy-start
